TPU v7x, 32 devices: a whole 2x2x4 slice. The times are simulated.
32 devices in a mesh: dp: 16 (over z, y, core), mp: 2 (over x).
Axes of the slice: x: 2, y: 2, z: 4, core: 2. Of those that a mesh axis runs over, the one named last changes fastest.
Arguments:
- tokens: bfloat16 [2304, 4096], P('dp'), may hold values from -6 to 6
- cotangent: bfloat16 [2304, 4096], P('dp'), may hold values from -6 to 6
- gate_blocks: bfloat16 [16, 128, 128], P('dp'), may hold values from -0.5 to 0.5
- up_blocks: bfloat16 [16, 128, 128], P('dp'), may hold values from -0.5 to 0.5
- down_blocks: bfloat16 [16, 128, 128], P('dp'), may hold values from -0.5 to 0.5
- col_block: int32 [16], replicated, may hold values from 0 to 223, as said below
- in_row: int32 [16], replicated, may hold values from 0 to 31, as said below
- out_row: int32 [16], replicated, may hold values from 0 to 31
Outputs:
- input_grad: bfloat16 [2304, 4096], P('dp', 'mp')
- gate_grads: float32 [16, 128, 128], P('dp')
- up_grads: float32 [16, 128, 128], P('dp')
- down_grads: float32 [16, 128, 128], P('dp')
Inputs may be any that keep to these rules, and one draw needn't show every extreme that they name: Flat blocks are ordered by owner: floor(col_block / 112) never falls along the list. Each owner holds 1 to 15 blocks, and some owner holds exactly 15. The pairs (in_row, col_block) are distinct, and so are the pairs (col_block, out_row). `in_row`: gate and up blocks share positions.
All inputs are finite; a program needn't handle non-finite values.
Results may differ from a plain program's by a relative error of at most 0.007.
Values may be sent and summed in bfloat16 or wider, within the bound.
No kernel may reach another device: no remote copies, remote signals or barrier semaphores. Data moves between devices by JAX's collectives and lax.ppermute only.
A program may use at most 64 MiB of HBM per device.

v0:
```python
import jax
import jax.numpy as jnp
from jax import lax
from jax.sharding import PartitionSpec as P

FF = 28672


def on_device(tokens, cotangent, gate_blocks, up_blocks, down_blocks, col_block, in_row, out_row):
    highest = lax.Precision.HIGHEST
    token_count = tokens.shape[0]
    model_width = tokens.shape[1]
    block_size = gate_blocks.shape[1]
    local_count = gate_blocks.shape[0]
    total_blocks = col_block.shape[0]
    model_count = lax.axis_size("mp")
    model_rank = lax.axis_index("mp")
    data_rank = lax.axis_index("dp")
    row_blocks = model_width // block_size
    owned_cols = FF // (block_size * model_count)
    capacity = min(20, total_blocks - model_count + 1)
    owner_of = col_block // owned_cols
    first_slot = jnp.sum((owner_of < model_rank).astype(jnp.int32))
    owned_count = jnp.sum((owner_of == model_rank).astype(jnp.int32))
    slot_ids = jnp.arange(capacity, dtype=jnp.int32)
    picked = jnp.minimum(first_slot + slot_ids, total_blocks - 1)
    live_slots = slot_ids < owned_count
    every_gate, every_up, every_down = (
        lax.all_gather(gate_blocks, "dp", axis=0, tiled=True),
        lax.all_gather(up_blocks, "dp", axis=0, tiled=True),
        lax.all_gather(down_blocks, "dp", axis=0, tiled=True),
    )

    def select_own(blocks_all):
        taken = jnp.take(blocks_all, picked, axis=0)
        return jnp.where(live_slots[:, None, None], taken, jnp.zeros((), blocks_all.dtype))

    own_gate = select_own(every_gate)
    own_up = select_own(every_up)
    own_down = select_own(every_down)
    columns = jnp.take(col_block, picked)
    rows_in = jnp.take(in_row, picked)
    rows_out = jnp.take(out_row, picked)
    same_column = (
        (columns[:, None] == columns[None, :]) & live_slots[:, None] & live_slots[None, :]
    ).astype(jnp.float32)
    token_in = jnp.take(tokens.reshape(token_count, row_blocks, block_size), rows_in, axis=1)
    cot_in = jnp.take(cotangent.reshape(token_count, row_blocks, block_size), rows_out, axis=1)
    gate_part = jnp.einsum("tkb,kbc->ktc", token_in, own_gate, preferred_element_type=jnp.float32)
    up_part = jnp.einsum("tkb,kbc->ktc", token_in, own_up, preferred_element_type=jnp.float32)
    gate_total = jnp.einsum("jk,ktc->jtc", same_column, gate_part, precision=highest)
    up_total = jnp.einsum("jk,ktc->jtc", same_column, up_part, precision=highest)
    gate_sigmoid = jax.nn.sigmoid(gate_total)
    gate_act = gate_total * gate_sigmoid
    hidden = (gate_act * up_total).astype(jnp.bfloat16)
    down_part = jnp.einsum("tkb,kcb->ktc", cot_in, own_down, preferred_element_type=jnp.float32)
    hidden_grad = jnp.einsum("jk,ktc->jtc", same_column, down_part, precision=highest)
    gate_grad = (
        hidden_grad * up_total * gate_sigmoid * (1.0 + gate_total * (1.0 - gate_sigmoid))
    ).astype(jnp.bfloat16)
    up_grad = (hidden_grad * gate_act).astype(jnp.bfloat16)
    grad_scale = (token_count * lax.axis_size("dp")) ** (-0.5)
    down_term = (
        jnp.einsum("ktc,tkb->kcb", hidden, cot_in, preferred_element_type=jnp.float32) * grad_scale
    )
    gate_term = (
        jnp.einsum("tkb,ktc->kbc", token_in, gate_grad, preferred_element_type=jnp.float32)
        * grad_scale
    )
    up_term = (
        jnp.einsum("tkb,ktc->kbc", token_in, up_grad, preferred_element_type=jnp.float32)
        * grad_scale
    )
    down_sum, gate_sum, up_sum = lax.psum((down_term, gate_term, up_term), "dp")
    flat_ids = data_rank * local_count + jnp.arange(local_count, dtype=jnp.int32)
    is_mine = jnp.take(owner_of, flat_ids) == model_rank
    flat_slot = jnp.clip(flat_ids - first_slot, 0, capacity - 1)

    def place_own(summed):
        return jnp.where(is_mine[:, None, None], jnp.take(summed, flat_slot, axis=0), 0.0)

    gate_flat, up_flat, down_flat = lax.psum(
        (place_own(gate_sum), place_own(up_sum), place_own(down_sum)), "mp"
    )
    spread = jnp.einsum("ktc,kbc->ktb", gate_grad, own_gate, preferred_element_type=jnp.float32)
    spread = spread + jnp.einsum(
        "ktc,kbc->ktb", up_grad, own_up, preferred_element_type=jnp.float32
    )
    row_onehot = (rows_in[:, None] == jnp.arange(row_blocks, dtype=jnp.int32)[None, :]).astype(
        jnp.float32
    )
    partial_value = jnp.einsum("kr,ktb->trb", row_onehot, spread, precision=highest).reshape(
        token_count, model_width
    )
    input_grad = lax.psum_scatter(
        partial_value.astype(jnp.bfloat16), "mp", scatter_dimension=1, tiled=True
    )
    return (input_grad, gate_flat, up_flat, down_flat)


def solution(mesh):
    return jax.shard_map(
        on_device,
        mesh=mesh,
        in_specs=(
            P("dp", None),
            P("dp", None),
            P("dp", None, None),
            P("dp", None, None),
            P("dp", None, None),
            P(),
            P(),
            P(),
        ),
        out_specs=(P("dp", "mp"), P("dp", None, None), P("dp", None, None), P("dp", None, None)),
        check_vma=False,
    )
```

profile of v0, /device:TPU:0, one launch (start us, length us, event | category | flops | bytes accessed | tf_op | source)
XLA Modules:
  0.0 262.1 jit_solution(15079879175695098051)
XLA Ops:
  7.2 1.4 fusion.46
  16.0 24.6 %all_gather.11 = bf16[16,128,128]{2,1,0:T(8,128)(2,1)S(1)} all-gather(bf16[1,128,128]{2,1,0:T(8,128)(2,1)S(1)} %copy-done.9), channel_id=1, replica_groups=mesh['dp'=16,'mp'=2] {'dp'}, dimensions={0}, use_global_device_ids=true | all-gather | bytes 557056 | tf_op jit(solution)/shard_map/all_gather | solution.py:29
  40.6 1.4 gather_fusion.7
  42.0 18.9 %all_gather.10 = bf16[16,128,128]{2,1,0:T(8,128)(2,1)S(1)} all-gather(bf16[1,128,128]{2,1,0:T(8,128)(2,1)S(1)} %copy-done.10), channel_id=1, replica_groups=mesh['dp'=16,'mp'=2] {'dp'}, dimensions={0}, use_global_device_ids=true | all-gather | bytes 557056 | tf_op jit(solution)/shard_map/all_gather | solution.py:30
  61.5 20.3 %all_gather.9 = bf16[16,128,128]{2,1,0:T(8,128)(2,1)S(1)} all-gather(bf16[1,128,128]{2,1,0:T(8,128)(2,1)S(1)} %copy-done.11), channel_id=1, replica_groups=mesh['dp'=16,'mp'=2] {'dp'}, dimensions={0}, use_global_device_ids=true | all-gather | bytes 557056 | tf_op jit(solution)/shard_map/all_gather | solution.py:31
  84.1 1.5 fusion.10
  85.7 1.5 fusion.12
  87.4 2.0 fusion.1
  90.1 1.6 fusion.15
  93.2 1.6 multiply_convert_fusion
  94.9 1.5 convolution_multiply_fusion
  96.4 1.5 convolution_multiply_fusion.1
  97.9 1.5 convolution_multiply_fusion.2
  102.6 97.5 %all-reduce.5.cloned.1.call-done = (f32[15,128,128]{2,1,0:T(8,128)}, f32[15,128,128]{2,1,0:T(8,128)}, f32[15,128,128]{2,1,0:T(8,128)}) async-done(((f32[15,128,128]{2,1,0:T(8,128)}, f32[15,128,128]{2,1,0:T(8,128)}, f32[15,128,128]{2,1,0:T(8,128)}), (f32[15,128,128]{2,1,0:T(8,128)}, f32[15,128,128]{2,1,0:T(8,128)}, f32[15,128,128]{2,1,0:T(8,128)})) %all-reduce.5.cloned.1.call-update) | async-done | bytes 2949136 | tf_op jit(solution)/shard_map/psum | solution.py:74
  200.1 1.5 select_select_fusion.6
  201.6 1.5 select_select_fusion.5
  203.1 1.5 select_select_fusion.4
  204.6 1.4 convolution_convert_fusion
  206.1 1.5 copy.66
  207.6 18.8 %all-reduce.7.cloned.1.call-done = (f32[1,128,128]{2,1,0:T(8,128)}, f32[1,128,128]{2,1,0:T(8,128)}, f32[1,128,128]{2,1,0:T(8,128)}) async-done(((f32[1,128,128]{2,1,0:T(8,128)}, f32[1,128,128]{2,1,0:T(8,128)}, f32[1,128,128]{2,1,0:T(8,128)}), (f32[1,128,128]{2,1,0:T(8,128)}, f32[1,128,128]{2,1,0:T(8,128)}, f32[1,128,128]{2,1,0:T(8,128)})) %all-reduce.7.cloned.1.call-update) | async-done | bytes 196624 | tf_op jit(solution)/shard_map/psum | solution.py:82
  226.4 24.7 %reduce-scatter.2.cloned.1.call-done = bf16[144,2048]{1,0:T(8,128)(2,1)} async-done(((bf16[144,4096]{1,0:T(8,128)(2,1)}), bf16[144,2048]{1,0:T(8,128)(2,1)}) %reduce-scatter.2.cloned.1.call-update) | async-done | bytes 589840 | tf_op jit(solution)/shard_map/reduce_scatter | solution.py:95
  251.1 1.5 copy.73
  252.6 1.5 copy.74
  254.1 1.5 copy.75
  (54 shorter events, 14.5 us)
Async XLA Ops:
  7.2 76.1 %copy-start = (bf16[144,4096]{1,0:T(8,128)(2,1)S(1)}, bf16[144,4096]{1,0:T(8,128)(2,1)}, u32[]{:S(2)}) copy-start(bf16[144,4096]{1,0:T(8,128)(2,1)} %param.16) | copy-start | bytes 3538948
  7.2 6.1 %copy-start.1 = (s32[16]{0:T(128)S(1)}, s32[16]{0:T(128)}, u32[]{:S(2)}) copy-start(s32[16]{0:T(128)} %param.23) | copy-start | bytes 196
  7.2 8.8 %copy-start.9 = (bf16[1,128,128]{2,1,0:T(8,128)(2,1)S(1)}, bf16[1,128,128]{2,1,0:T(8,128)(2,1)}, u32[]{:S(2)}) copy-start(bf16[1,128,128]{2,1,0:T(8,128)(2,1)} %param.18) | copy-start | bytes 98308
  7.2 192.9 %all-reduce.5.cloned.1.call-start = ((), (), s32[]{:S(2)}) async-start(), calls=%async_computation.2 | async-start | bytes 5898240 | tf_op jit(solution)/shard_map/psum | solution.py:74
  11.9 30.1 %copy-start.10 = (bf16[1,128,128]{2,1,0:T(8,128)(2,1)S(1)}, bf16[1,128,128]{2,1,0:T(8,128)(2,1)}, u32[]{:S(2)}) copy-start(bf16[1,128,128]{2,1,0:T(8,128)(2,1)} %param.19) | copy-start | bytes 98308
  40.6 20.9 %copy-start.11 = (bf16[1,128,128]{2,1,0:T(8,128)(2,1)S(1)}, bf16[1,128,128]{2,1,0:T(8,128)(2,1)}, u32[]{:S(2)}) copy-start(bf16[1,128,128]{2,1,0:T(8,128)(2,1)} %param.20) | copy-start | bytes 98308
  61.5 24.1 %copy-start.4 = (bf16[15,128,128]{2,1,0:T(8,128)(2,1)}, bf16[15,128,128]{2,1,0:T(8,128)(2,1)S(1)}, u32[]{:S(2)}) copy-start(bf16[15,128,128]{2,1,0:T(8,128)(2,1)S(1)} %gather_fusion.6) | copy-start | bytes 1474564
  85.7 1.5 copy-start.7
  91.6 1.3 copy-start.8
  91.6 1.6 copy-start.12
  94.9 3.0 %copy-start.2 = (bf16[15,144,128]{2,0,1:T(8,128)(2,1)}, bf16[15,144,128]{2,0,1:T(8,128)(2,1)S(1)}, u32[]{:S(2)}) copy-start(bf16[15,144,128]{2,0,1:T(8,128)(2,1)S(1)} %get-tuple-element.44) | copy-start | bytes 1658884
  99.4 2.1 copy-start.3
  99.4 2.1 copy-start.6
  99.5 2.6 copy-start.5
  99.5 127.0 %all-reduce.7.cloned.1.call-start = ((), (), s32[]{:S(2)}) async-start(), calls=%async_computation.3 | async-start | bytes 393216 | tf_op jit(solution)/shard_map/psum | solution.py:82
  204.6 46.5 %reduce-scatter.2.cloned.1.call-start = ((), (), s32[]{:S(2)}) async-start(), calls=%async_computation.1 | async-start | bytes 1769472 | tf_op jit(solution)/shard_map/reduce_scatter | solution.py:95
Sparse Core Ops, SparseCore 0:
  99.6 100.4 all-reduce.4
  204.7 21.6 all-reduce.6
  229.3 21.8 reduce-scatter.1
where the time goes:
time: 263 us; the launch traced here: 262 us
  waiting for transfers between devices  141 us (54%)
  blocking collectives  63.8 us (24%)
  matrix products  16.3 us (6%)
  local copies, waits for them, and re-layouts  15.6 us (6%)
  between operations  15.4 us (6%)
  other arithmetic  9.77 us (4%)
    psum x1, waiting for transfers between devices, on_device(): down_sum, gate_sum, up_sum = lax.psum((down_term, gate_term, up_term), 'dp')  97.5 us
    reduce_scatter x1, waiting for transfers between devices, on_device(): lax.psum_scatter(partial_value.astype(jnp.bfloat16), 'mp', scatter_dimens...  24.7 us
    all_gather x1, blocking collectives, on_device(): lax.all_gather(gate_blocks, 'dp', axis=0, tiled=True)  24.6 us
    all_gather x1, blocking collectives, on_device(): lax.all_gather(down_blocks, 'dp', axis=0, tiled=True)  20.3 us
    all_gather x1, blocking collectives, on_device(): lax.all_gather(up_blocks, 'dp', axis=0, tiled=True)  18.9 us
    psum x1, waiting for transfers between devices, on_device(): lax.psum((place_own(gate_sum), place_own(up_sum), place_own(down_sum)), '...  18.8 us
    unnamed x30, local copies, waits for them, and re-layouts  6.59 us
  transfers between devices with their start and end apart: 3, of which 3 were waited for; matrix products, arithmetic and copies ran while one was open for 2% of the time, Pallas kernels for 0%

commit v1 on v0

v1 whole, which is shorter than its diff:
```python
import functools

import jax
import jax.numpy as jnp
from jax import lax
from jax.experimental import pallas as pl
from jax.experimental.pallas import tpu as pltpu
from jax.sharding import PartitionSpec as P

VMEM = pltpu.MemorySpace.VMEM
SMEM = pltpu.MemorySpace.SMEM
F32 = jnp.float32
BF16 = jnp.bfloat16


def dot(a, b, dim_a, dim_b):
    return lax.dot_general(a, b, (((dim_a,), (dim_b,)), ((), ())), preferred_element_type=F32)


def repeat(count, body):
    if count <= 16:
        for i in range(count):
            body(i)
    else:

        def step(i, carry):
            body(i)
            return carry

        lax.fori_loop(0, count, step, 0)


def pack_kernel(rank_ref, gate_ref, up_ref, down_ref, out_ref, turned):
    share = out_ref.shape[1] // 3
    first = pl.multiple_of(rank_ref[0] * share, share)
    for i in range(gate_ref.shape[0]):
        turned[...] = gate_ref[i].astype(F32).T
        out_ref[i, :share] = turned[pl.ds(first, share), :].astype(BF16)
        turned[...] = up_ref[i].astype(F32).T
        out_ref[i, share : 2 * share] = turned[pl.ds(first, share), :].astype(BF16)
        turned[...] = down_ref[i].astype(F32)
        out_ref[i, 2 * share :] = turned[pl.ds(first, share), :].astype(BF16)


def layer_kernel(rank_ref, col_ref, in_ref, out_row_ref, tok_ref, cot_ref, w_ref, *rest, ranks):
    spread_refs, (grad_ref, gu, dh, gu_grad, hidden, total) = rest[:ranks], rest[ranks:]
    count, rows, block = w_ref.shape
    share = rows // 3
    two = 2 * share
    rank = rank_ref[0]

    def columns(ref, index):
        return ref[:, pl.ds(pl.multiple_of(index * block, block), block)]

    def leader(k):
        return lax.fori_loop(
            0, k, lambda j, best: jnp.where(col_ref[k - 1 - j] == col_ref[k], k - 1 - j, best), k
        )

    def forward(k):
        gu[k] = dot(w_ref[k, :two], columns(tok_ref, in_ref[k]), 1, 1)
        dh[k] = dot(w_ref[k, two:], columns(cot_ref, out_row_ref[k]), 1, 1)

    repeat(count, forward)
    total[...] = jnp.zeros_like(total)
    heads = [leader(k) for k in range(count)] if count <= 16 else None

    def head(k):
        return heads[k] if heads is not None else leader(k)

    def join(k):
        first = head(k)

        @pl.when(first != k)
        def _():
            gu[first] += gu[k]
            dh[first] += dh[k]

    repeat(count, join)

    def middle(k):
        gate, up, grad = gu[k, :share], gu[k, share:], dh[k]
        sig = jax.nn.sigmoid(gate)
        act = gate * sig
        hidden[k] = (act * up).astype(BF16)
        gu_grad[k, :share] = (grad * up * sig * (1.0 + gate * (1.0 - sig))).astype(BF16)
        gu_grad[k, share:] = (grad * act).astype(BF16)

    repeat(count, middle)

    def spread(k):
        total[in_ref[k]] += dot(gu_grad[head(k)], w_ref[k, :two], 0, 0)

    repeat(count, spread)
    for d in range(ranks):
        per = total.shape[0] // ranks
        for r in range(per):
            spread_refs[d][:, r * block : (r + 1) * block] = total[(rank ^ d) * per + r].astype(BF16)

    def backward(k):
        first = head(k)
        grad_ref[k, :two] = dot(gu_grad[first], columns(tok_ref, in_ref[k]), 1, 0).astype(BF16)
        grad_ref[k, two:] = dot(hidden[first], columns(cot_ref, out_row_ref[k]), 1, 0).astype(BF16)

    repeat(count, backward)


def sum_kernel(parts_ref, out_ref, *, scale):
    total = parts_ref[0].astype(F32)
    for i in range(1, parts_ref.shape[0]):
        total += parts_ref[i].astype(F32)
    out_ref[...] = total * scale


def place_kernel(rank_ref, *refs, ranks):
    pieces, (gate_ref, up_ref, down_ref, whole) = refs[:ranks], refs[ranks:]
    share = pieces[0].shape[1] // 3
    for i in range(gate_ref.shape[0]):
        for part, ref in enumerate((gate_ref, up_ref, down_ref)):
            for d in range(ranks):
                at = pl.multiple_of((rank_ref[0] ^ d) * share, share)
                whole[pl.ds(at, share), :] = pieces[d][i, part * share : (part + 1) * share]
            ref[i] = whole[...] if part == 2 else whole[...].T


def call(kernel, out_shape, scalars, arrays, scratch=()):
    return pl.pallas_call(
        kernel,
        out_shape=out_shape,
        in_specs=[pl.BlockSpec(memory_space=SMEM)] * scalars + [pl.BlockSpec(memory_space=VMEM)] * arrays,
        out_specs=jax.tree.map(lambda _: pl.BlockSpec(memory_space=VMEM), out_shape),
        scratch_shapes=list(scratch),
    )


def on_device(tokens, cotangent, gate_blocks, up_blocks, down_blocks, col_block, in_row, out_row):
    shape = jax.ShapeDtypeStruct
    token_count, width = tokens.shape
    local, block, _ = gate_blocks.shape
    count = col_block.shape[0]
    groups, ranks = lax.axis_size("dp"), lax.axis_size("mp")
    share = block // ranks
    rank = lax.axis_index("mp").astype(jnp.int32).reshape(1)
    scale = (token_count * groups) ** -0.5

    own = call(
        pack_kernel, shape((local, 3 * share, block), BF16), 1, 3, [pltpu.VMEM((block, block), F32)]
    )(rank, gate_blocks, up_blocks, down_blocks)
    weights = lax.all_gather(own, "dp", axis=0, tiled=True)
    *spread, grads = call(
        functools.partial(layer_kernel, ranks=ranks),
        [shape((token_count, width // ranks), BF16)] * ranks + [shape((count, 3 * share, block), BF16)],
        4,
        3,
        [
            pltpu.VMEM((count, 2 * share, token_count), F32),
            pltpu.VMEM((count, share, token_count), F32),
            pltpu.VMEM((count, 2 * share, token_count), BF16),
            pltpu.VMEM((count, share, token_count), BF16),
            pltpu.VMEM((width // block, token_count, block), F32),
        ],
    )(rank, col_block, in_row, out_row, tokens, cotangent, weights)

    def across(x, d):
        return lax.ppermute(x, "mp", [(i, i ^ d) for i in range(ranks)])

    arrived = [across(spread[d], d) for d in range(1, ranks)]
    parts = lax.all_to_all(
        grads.reshape(groups, local * 3 * share, block), "dp", 0, 0, tiled=True
    ).reshape(groups, local, 3 * share, block)
    summed = call(functools.partial(sum_kernel, scale=scale), shape((local, 3 * share, block), F32), 0, 1)(parts)
    pieces = [summed] + [across(summed, d) for d in range(1, ranks)]
    grad_shape = shape((local, block, block), F32)
    gate_grads, up_grads, down_grads = call(
        functools.partial(place_kernel, ranks=ranks),
        [grad_shape] * 3,
        1,
        ranks,
        [pltpu.VMEM((block, block), F32)],
    )(rank, *pieces)
    input_grad = spread[0].astype(F32)
    for piece in arrived:
        input_grad = input_grad + piece.astype(F32)
    return input_grad.astype(BF16), gate_grads, up_grads, down_grads


def solution(mesh):
    flat = P("dp", None, None)
    return jax.shard_map(
        on_device,
        mesh=mesh,
        in_specs=(P("dp", None), P("dp", None), flat, flat, flat, P(), P(), P()),
        out_specs=(P("dp", "mp"), flat, flat, flat),
        check_vma=False,
    )
```

time: 263 us -> 68.7 us (0.26)
  waiting for transfers between devices: 141 us -> 19.8 us
  blocking collectives: 63.8 us -> 27 us
  matrix products: 16.3 us -> 0 us
  between operations: 15.4 us -> 0.66 us
  local copies, waits for them, and re-layouts: 15.6 us -> 1.52 us
  Pallas kernels: 0 us -> 11.6 us
  other arithmetic: 9.77 us -> 0.97 us
  starting transfers between devices: 0.12 us -> 6.8 us
    psum x2 -> x0, waiting for transfers between devices: 116 us -> none  [the longest x1 97.5 us: on_device(): down_sum, gate_sum, up_sum = lax.psum((down_term, gate_term, up_term), 'dp')]
    all_gather x3 -> x1, blocking collectives: 63.8 us -> 27 us  [on_device(): weights = lax.all_gather(own, 'dp', axis=0, tiled=True)]
    reduce_scatter x1 -> x0, waiting for transfers between devices: 24.7 us -> none  [on_device(): lax.psum_scatter(partial_value.astype(jnp.bfloat16), 'mp', scatter_dimens...]
    all_to_all x0 -> x1, waiting for transfers between devices: none -> 17.1 us  [on_device(): lax.all_to_all(grads.reshape(groups, local * 3 * share, block), 'dp', 0,...]
    dot_general x12 -> x0, matrix products: 16.3 us -> none  [the longest x1 2.03 us: on_device(): jnp.einsum('jk,ktc->jtc', same_column, gate_part, precision=highest)]
    pallas_call x0 -> x4, Pallas kernels: none -> 11.6 us  [the longest x1 6.41 us: on_device(): call(functools.partial(layer_kernel, ranks=ranks), [shape((token_count, w...]
    gather x9 -> x0, local copies, waits for them, and re-layouts: 8.63 us -> none  [the longest x3 3.43 us: select_own(): taken = jnp.take(blocks_all, picked, axis=0)]
    select_n x6 -> x0, other arithmetic: 5.74 us -> none  [the longest x3 4.43 us: place_own(): jnp.where(is_mine[:, None, None], jnp.take(summed, flat_slot, axis=0), 0.0)]
  transfers between devices with their start and end apart: 3 -> 3, of which waited for: 3 -> 2; matrix products, arithmetic and copies ran while one was open for 2% -> 1% of each run, Pallas kernels for 0% -> 3%
where the time goes in v1:
time: 68.7 us; the launch traced here: 68.3 us
  blocking collectives  27 us (39%)
  waiting for transfers between devices  19.8 us (29%)
  Pallas kernels  11.6 us (17%)
  starting transfers between devices  6.8 us (10%)
  local copies, waits for them, and re-layouts  1.52 us (2%)
  other arithmetic  0.97 us (1%)
    all_gather x1, blocking collectives, on_device(): weights = lax.all_gather(own, 'dp', axis=0, tiled=True)  27 us
    all_to_all x1, waiting for transfers between devices, on_device(): lax.all_to_all(grads.reshape(groups, local * 3 * share, block), 'dp', 0,...  17.1 us
    pallas_call x1, Pallas kernels, on_device(): call(functools.partial(layer_kernel, ranks=ranks), [shape((token_count, w...  6.41 us
    all_to_all x1, starting transfers between devices, on_device(): lax.all_to_all(grads.reshape(groups, local * 3 * share, block), 'dp', 0,...  3.74 us
    ppermute x2, starting transfers between devices, across(): return lax.ppermute(x, 'mp', [(i, i ^ d) for i in range(ranks)])  3.06 us
    ppermute x2, waiting for transfers between devices, across(): return lax.ppermute(x, 'mp', [(i, i ^ d) for i in range(ranks)])  2.77 us
    pallas_call x1, Pallas kernels, on_device(): call(functools.partial(sum_kernel, scale=scale), shape((local, 3 * share,...  1.89 us
    pallas_call x1, Pallas kernels, on_device(): call(functools.partial(place_kernel, ranks=ranks), [grad_shape] * 3, 1, r...  1.72 us
  transfers between devices with their start and end apart: 3, of which 2 were waited for; matrix products, arithmetic and copies ran while one was open for 1% of the time, Pallas kernels for 3%

profile of v1, /device:TPU:0, one launch (start us, length us, event | category | flops | bytes accessed | tf_op | source)
XLA Modules:
  0.0 68.3 jit_solution(7704518380734080415)
XLA Ops:
  0.6 1.5 %shard_map.111 = bf16[1,192,128]{2,1,0:T(8,128)(2,1)} custom-call(s32[1]{0:T(128)} %bitcast.rank_ref, bf16[1,128,128]{2,1,0:T(8,128)(2,1)} %gate_ref.1, bf16[1,128,128]{2,1,0:T(8,128)(2,1)} %up_ref.1, bf16[1,128,128]{2,1,0:T(8,128)(2,1)} %down_ref.1), custom_call_target="tpu_custom_call" | custom-call | tf_op jit(solution)/shard_map/pallas_call | solution.py:146
  2.2 27.0 %all_gather.3.w_ref = bf16[16,192,128]{2,1,0:T(8,128)(2,1)} all-gather(bf16[1,192,128]{2,1,0:T(8,128)(2,1)} %shard_map.111), channel_id=1, replica_groups=mesh['dp'=16,'mp'=2] {'dp'}, dimensions={0}, use_global_device_ids=true | all-gather | bytes 835584 | tf_op jit(solution)/shard_map/all_gather | solution.py:149
  29.2 6.4 %shard_map.112 = (bf16[144,2048]{1,0:T(8,128)(2,1)}, bf16[144,2048]{1,0:T(8,128)(2,1)}, bf16[16,192,128]{2,1,0:T(8,128)(2,1)}) custom-call(s32[1]{0:T(128)} %bitcast.rank_ref, s32[16]{0:T(128)} %col_ref.1, s32[16]{0:T(128)} %in_ref.1, s32[16]{0:T(128)} %out_row_ref.1, bf16[144,4096]{1,0:T(8,128)(2,1)} %tok_ref.1, bf16[144,4096]{1,0:T(8,128)(2,1)} %cot_ref.1, ...), custom_call_target="tpu_custom_call" | custom-call | tf_op jit(solution)/shard_map/pallas_call | solution.py:150
  35.6 0.0 copy-start.3
  35.6 0.0 copy-start.1
  35.6 3.7 %all-to-all-start = ((bf16[16,192,128]{2,1,0:T(8,128)(2,1)}), bf16[16,192,128]{2,1,0:T(8,128)(2,1)S(1)}, u32[]{:S(2)}, u32[]{:S(2)}) async-start(bf16[16,192,128]{2,1,0:T(8,128)(2,1)} %get-tuple-element.12), calls=%async_computation | async-start | bytes 1572864 | tf_op jit(solution)/shard_map/all_to_all | solution.py:168
  39.3 0.0 copy-done.3
  39.3 1.6 %collective-permute-start = (bf16[144,2048]{1,0:T(8,128)(2,1)S(1)}, bf16[144,2048]{1,0:T(8,128)(2,1)S(1)}, u32[]{:S(2)}, u32[]{:S(2)}) collective-permute-start(bf16[144,2048]{1,0:T(8,128)(2,1)S(1)} %copy-done.3), channel_id=1, source_target_pairs={{0,1},{1,0},{2,3},{3,2},{4,5},{5,4},{6,7},{7,6},{8,9},{9,8},{10,11... | collective-permute-start | bytes 1769480 | tf_op jit(solution)/shard_map/ppermute | solution.py:165
  40.9 17.1 %all-to-all-done = bf16[16,192,128]{2,1,0:T(8,128)(2,1)S(1)} async-done(((bf16[16,192,128]{2,1,0:T(8,128)(2,1)}), bf16[16,192,128]{2,1,0:T(8,128)(2,1)S(1)}, u32[]{:S(2)}, u32[]{:S(2)}) %all-to-all-start) | async-done | bytes 786464 | tf_op jit(solution)/shard_map/all_to_all | solution.py:168
  58.0 0.0 copy-start
  58.0 0.9 %copy-done = bf16[16,192,128]{2,1,0:T(8,128)(2,1)} copy-done((bf16[16,192,128]{2,1,0:T(8,128)(2,1)}, bf16[16,192,128]{2,1,0:T(8,128)(2,1)S(1)}, u32[]{:S(2)}) %copy-start) | copy-done | bytes 786456
  58.8 1.9 %shard_map.113.refs_0_ = f32[1,192,128]{2,1,0:T(8,128)} custom-call(bf16[16,1,192,128]{3,2,1,0:T(8,128)(2,1)} %bitcast.2), custom_call_target="tpu_custom_call" | custom-call | tf_op jit(solution)/shard_map/pallas_call | solution.py:171
  60.7 1.5 %collective-permute-start.1 = (f32[1,192,128]{2,1,0:T(8,128)}, f32[1,192,128]{2,1,0:T(8,128)S(1)}, u32[]{:S(2)}, u32[]{:S(2)}) collective-permute-start(f32[1,192,128]{2,1,0:T(8,128)} %shard_map.113.refs_0_), channel_id=1, source_target_pairs={{0,1},{1,0},{2,3},{3,2},{4,5},{5,4},{6,7},{7,6},{8,9},{9,8},{10,11... | collective-permute-start | bytes 294920 | tf_op jit(solution)/shard_map/ppermute | solution.py:165
  62.2 0.0 collective-permute-done
  62.2 0.0 copy-done.1
  62.2 1.0 %add_convert_fusion = bf16[144,2048]{1,0:T(8,128)(2,1)} fusion(bf16[144,2048]{1,0:T(8,128)(2,1)S(1)} %collective-permute-done, bf16[144,2048]{1,0:T(8,128)(2,1)S(1)} %copy-done.1), kind=kLoop, calls=%fused_computation | loop fusion | flops 1179648 | bytes 1769472 | tf_op jit(solution)/shard_map/convert_element_type | solution.py:184
  63.2 2.8 %collective-permute-done.1.refs_1_ = f32[1,192,128]{2,1,0:T(8,128)S(1)} collective-permute-done((f32[1,192,128]{2,1,0:T(8,128)}, f32[1,192,128]{2,1,0:T(8,128)S(1)}, u32[]{:S(2)}, u32[]{:S(2)}) %collective-permute-start.1) | collective-permute-done | bytes 98336 | tf_op jit(solution)/shard_map/ppermute | solution.py:165
  66.0 0.0 copy-start.2
  66.0 0.6 copy-done.2
  66.6 1.7 %shard_map.114 = (f32[1,128,128]{2,1,0:T(8,128)}, f32[1,128,128]{2,1,0:T(8,128)}, f32[1,128,128]{2,1,0:T(8,128)}) custom-call(s32[1]{0:T(128)} %bitcast.rank_ref, f32[1,192,128]{2,1,0:T(8,128)} %shard_map.113.refs_0_, f32[1,192,128]{2,1,0:T(8,128)} %copy-done.2), custom_call_target="tpu_custom_call" | custom-call | tf_op jit(solution)/shard_map/pallas_call | solution.py:174
Async XLA Ops:
  35.6 3.8 %copy-start.3 = (bf16[144,2048]{1,0:T(8,128)(2,1)S(1)}, bf16[144,2048]{1,0:T(8,128)(2,1)}, u32[]{:S(2)}) copy-start(bf16[144,2048]{1,0:T(8,128)(2,1)} %get-tuple-element.11) | copy-start | bytes 1769476
  35.6 26.7 %copy-start.1 = (bf16[144,2048]{1,0:T(8,128)(2,1)S(1)}, bf16[144,2048]{1,0:T(8,128)(2,1)}, u32[]{:S(2)}) copy-start(bf16[144,2048]{1,0:T(8,128)(2,1)} %get-tuple-element.10) | copy-start | bytes 1769476
  35.6 22.4 %all-to-all-start = ((bf16[16,192,128]{2,1,0:T(8,128)(2,1)}), bf16[16,192,128]{2,1,0:T(8,128)(2,1)S(1)}, u32[]{:S(2)}, u32[]{:S(2)}) async-start(bf16[16,192,128]{2,1,0:T(8,128)(2,1)} %get-tuple-element.12), calls=%async_computation | async-start | bytes 1572864 | tf_op jit(solution)/shard_map/all_to_all | solution.py:168
  39.3 22.9 %collective-permute-start = (bf16[144,2048]{1,0:T(8,128)(2,1)S(1)}, bf16[144,2048]{1,0:T(8,128)(2,1)S(1)}, u32[]{:S(2)}, u32[]{:S(2)}) collective-permute-start(bf16[144,2048]{1,0:T(8,128)(2,1)S(1)} %copy-done.3), channel_id=1, source_target_pairs={{0,1},{1,0},{2,3},{3,2},{4,5},{5,4},{6,7},{7,6},{8,9},{9,8},{10,11... | collective-permute-start | bytes 1769480 | tf_op jit(solution)/shard_map/ppermute | solution.py:165
  58.0 0.9 %copy-start = (bf16[16,192,128]{2,1,0:T(8,128)(2,1)}, bf16[16,192,128]{2,1,0:T(8,128)(2,1)S(1)}, u32[]{:S(2)}) copy-start(bf16[16,192,128]{2,1,0:T(8,128)(2,1)S(1)} %all-to-all-done) | copy-start | bytes 2359300
  60.7 5.2 %collective-permute-start.1 = (f32[1,192,128]{2,1,0:T(8,128)}, f32[1,192,128]{2,1,0:T(8,128)S(1)}, u32[]{:S(2)}, u32[]{:S(2)}) collective-permute-start(f32[1,192,128]{2,1,0:T(8,128)} %shard_map.113.refs_0_), channel_id=1, source_target_pairs={{0,1},{1,0},{2,3},{3,2},{4,5},{5,4},{6,7},{7,6},{8,9},{9,8},{10,11... | collective-permute-start | bytes 294920 | tf_op jit(solution)/shard_map/ppermute | solution.py:165
  66.0 0.6 copy-start.2

commit v2 on v1

v2 whole, which is shorter than its diff:
```python
import functools

import jax
import jax.numpy as jnp
from jax import lax
from jax.experimental import pallas as pl
from jax.experimental.pallas import tpu as pltpu
from jax.sharding import PartitionSpec as P

VMEM = pltpu.MemorySpace.VMEM
SMEM = pltpu.MemorySpace.SMEM
F32 = jnp.float32
BF16 = jnp.bfloat16


def dot(a, b, dim_a, dim_b):
    return lax.dot_general(a, b, (((dim_a,), (dim_b,)), ((), ())), preferred_element_type=F32)


def pack_kernel(rank_ref, gate_ref, up_ref, down_ref, out_ref, turned):
    share = out_ref.shape[1] // 3
    first = pl.multiple_of(rank_ref[0] * share, share)
    for i in range(gate_ref.shape[0]):
        turned[...] = gate_ref[i].astype(F32).T
        out_ref[i, :share] = turned[pl.ds(first, share), :].astype(BF16)
        turned[...] = up_ref[i].astype(F32).T
        out_ref[i, share : 2 * share] = turned[pl.ds(first, share), :].astype(BF16)
        turned[...] = down_ref[i].astype(F32)
        out_ref[i, 2 * share :] = turned[pl.ds(first, share), :].astype(BF16)


def layer_kernel(place_ref, col_ref, in_ref, out_row_ref, tok_ref, cot_ref, near_ref, far_ref, *rest, ranks, local):
    spread_refs, (near_grad, far_grad, gu, dh, gu_grad, hidden, total) = rest[:ranks], rest[ranks:]
    half, rows, block = near_ref.shape
    count = 2 * half
    share = rows // 3
    two = 2 * share
    me, rank = place_ref[0], place_ref[1]
    quarter = half // local // 2

    def flat(slot):
        at, inner = slot // local, slot % local
        side, pair, far = at // (2 * quarter), (at // quarter) % 2, at % quarter
        return (me ^ (far * 4 + pair * 2 + side)) * local + inner

    def weight(slot, first, last):
        return (near_ref if slot < half else far_ref)[slot % half, first:last]

    def columns(ref, index):
        return ref[:, pl.ds(pl.multiple_of(index * block, block), block)]

    keys = [flat(slot) for slot in range(count)]
    cols = [col_ref[key] for key in keys]
    rows_in = [in_ref[key] for key in keys]
    rows_out = [out_row_ref[key] for key in keys]
    heads = []
    for slot in range(count):
        best = jnp.int32(slot)
        for earlier in reversed(range(slot)):
            best = jnp.where(cols[earlier] == cols[slot], earlier, best)
        heads.append(best)

    for slot in range(count):
        gu[slot] = dot(weight(slot, 0, two), columns(tok_ref, rows_in[slot]), 1, 1)
        dh[slot] = dot(weight(slot, two, rows), columns(cot_ref, rows_out[slot]), 1, 1)
    total[...] = jnp.zeros_like(total)
    for slot in range(1, count):

        @pl.when(heads[slot] != slot)
        def _(slot=slot):
            gu[heads[slot]] += gu[slot]
            dh[heads[slot]] += dh[slot]

    for slot in range(count):
        gate, up, grad = gu[slot, :share], gu[slot, share:], dh[slot]
        sig = jax.nn.sigmoid(gate)
        act = gate * sig
        hidden[slot] = (act * up).astype(BF16)
        gu_grad[slot, :share] = (grad * up * sig * (1.0 + gate * (1.0 - sig))).astype(BF16)
        gu_grad[slot, share:] = (grad * act).astype(BF16)
    for slot in range(count):
        total[rows_in[slot]] += dot(gu_grad[heads[slot]], weight(slot, 0, two), 0, 0)
    per = total.shape[0] // ranks
    for d in range(ranks):
        for r in range(per):
            spread_refs[d][:, r * block : (r + 1) * block] = total[(rank ^ d) * per + r].astype(BF16)
    for slot in range(count):
        ref, at = (near_grad if slot < half else far_grad), slot % half
        ref[at, :two] = dot(gu_grad[heads[slot]], columns(tok_ref, rows_in[slot]), 1, 0).astype(BF16)
        ref[at, two:] = dot(hidden[heads[slot]], columns(cot_ref, rows_out[slot]), 1, 0).astype(BF16)


def place_kernel(rank_ref, *refs, ranks):
    pieces, (gate_ref, up_ref, down_ref, whole) = refs[:ranks], refs[ranks:]
    share = pieces[0].shape[1] // 3
    for i in range(gate_ref.shape[0]):
        for part, ref in enumerate((gate_ref, up_ref, down_ref)):
            for d in range(ranks):
                at = pl.multiple_of((rank_ref[0] ^ d) * share, share)
                whole[pl.ds(at, share), :] = pieces[d][i, part * share : (part + 1) * share]
            ref[i] = whole[...] if part == 2 else whole[...].T


def call(kernel, out_shape, scalars, arrays, scratch=()):
    return pl.pallas_call(
        kernel,
        out_shape=out_shape,
        in_specs=[pl.BlockSpec(memory_space=SMEM)] * scalars + [pl.BlockSpec(memory_space=VMEM)] * arrays,
        out_specs=jax.tree.map(lambda _: pl.BlockSpec(memory_space=VMEM), out_shape),
        scratch_shapes=list(scratch),
    )


def on_device(tokens, cotangent, gate_blocks, up_blocks, down_blocks, col_block, in_row, out_row):
    shape = jax.ShapeDtypeStruct
    token_count, width = tokens.shape
    local, block, _ = gate_blocks.shape
    count = col_block.shape[0]
    groups, ranks = lax.axis_size("dp"), lax.axis_size("mp")
    share = block // ranks
    rank = lax.axis_index("mp").astype(jnp.int32).reshape(1)
    scale = (token_count * groups) ** -0.5

    def along(x, axis, size, d):
        return lax.ppermute(x, axis, [(i, i ^ d) for i in range(size)])

    def over(x, d):
        return along(x, "dp", groups, d)

    own = call(
        pack_kernel, shape((local, 3 * share, block), BF16), 1, 3, [pltpu.VMEM((block, block), F32)]
    )(rank, gate_blocks, up_blocks, down_blocks)
    fars = groups // 4
    quarter = fars * local
    column = jnp.concatenate([own] + [over(own, 4 * i) for i in range(1, fars)], axis=0)
    near = jnp.concatenate([column, over(column, 2)], axis=0)
    far = over(near, 1)
    place = jnp.concatenate([lax.axis_index("dp").astype(jnp.int32).reshape(1), rank])
    grad_parts = shape((2 * quarter, 3 * share, block), BF16)
    *spread, near_grad, far_grad = call(
        functools.partial(layer_kernel, ranks=ranks, local=local),
        [shape((token_count, width // ranks), BF16)] * ranks + [grad_parts] * 2,
        4,
        4,
        [
            pltpu.VMEM((count, 2 * share, token_count), F32),
            pltpu.VMEM((count, share, token_count), F32),
            pltpu.VMEM((count, 2 * share, token_count), BF16),
            pltpu.VMEM((count, share, token_count), BF16),
            pltpu.VMEM((width // block, token_count, block), F32),
        ],
    )(place, col_block, in_row, out_row, tokens, cotangent, near, far)

    def across(x, d):
        return along(x, "mp", ranks, d)

    arrived = [across(spread[d], d) for d in range(1, ranks)]
    chip = near_grad.astype(F32) + over(far_grad, 1).astype(F32)
    plane = chip[:quarter] + over(chip[quarter:].astype(BF16), 2).astype(F32)
    summed = plane[:local]
    for i in range(1, fars):
        piece = plane[i * local : (i + 1) * local].astype(BF16)
        summed = summed + over(piece, 4 * i).astype(F32)
    summed = summed * scale
    pieces = [summed] + [across(summed, d) for d in range(1, ranks)]
    grad_shape = shape((local, block, block), F32)
    gate_grads, up_grads, down_grads = call(
        functools.partial(place_kernel, ranks=ranks),
        [grad_shape] * 3,
        1,
        ranks,
        [pltpu.VMEM((block, block), F32)],
    )(rank, *pieces)
    input_grad = spread[0].astype(F32)
    for piece in arrived:
        input_grad = input_grad + piece.astype(F32)
    return input_grad.astype(BF16), gate_grads, up_grads, down_grads


def solution(mesh):
    flat = P("dp", None, None)
    return jax.shard_map(
        on_device,
        mesh=mesh,
        in_specs=(P("dp", None), P("dp", None), flat, flat, flat, P(), P(), P()),
        out_specs=(P("dp", "mp"), flat, flat, flat),
        check_vma=False,
    )
```

time: 68.7 us -> 53.4 us (0.78)
  blocking collectives: 27 us -> 0 us
  starting transfers between devices: 6.8 us -> 15.6 us
  Pallas kernels: 11.6 us -> 8.88 us
  other arithmetic: 0.97 us -> 3.54 us
  waiting for transfers between devices: 19.8 us -> 21.9 us
  local copies, waits for them, and re-layouts: 1.52 us -> 2.35 us
    all_gather x1 -> x0, blocking collectives: 27 us -> none  [on_device(): weights = lax.all_gather(own, 'dp', axis=0, tiled=True)]
    ppermute x2 -> x12, waiting for transfers between devices: 2.77 us -> 21.9 us  [along(): return lax.ppermute(x, axis, [(i, i ^ d) for i in range(size)])]
    all_to_all x1 -> x0, waiting for transfers between devices: 17.1 us -> none  [on_device(): lax.all_to_all(grads.reshape(groups, local * 3 * share, block), 'dp', 0,...]
    ppermute x2 -> x12, starting transfers between devices: 3.06 us -> 15.6 us  [along(): return lax.ppermute(x, axis, [(i, i ^ d) for i in range(size)])]
    all_to_all x1 -> x0, starting transfers between devices: 3.74 us -> none  [on_device(): lax.all_to_all(grads.reshape(groups, local * 3 * share, block), 'dp', 0,...]
    pallas_call x2 -> x1, Pallas kernels: 8.31 us -> 5.63 us  [on_device(): call(functools.partial(layer_kernel, ranks=ranks, local=local), [shape((t...]
    concatenate x0 -> x2, other arithmetic: none -> 1.41 us  [the longest x1 0.83 us: on_device(): jnp.concatenate([own] + [over(own, 4 * i) for i in range(1, fars)], axis=0)]
    add x0 -> x1, other arithmetic: none -> 1.08 us  [on_device(): chip = near_grad.astype(F32) + over(far_grad, 1).astype(F32)]
  transfers between devices with their start and end apart: 3 -> 12, of which waited for: 2 -> 10; matrix products, arithmetic and copies ran while one was open for 1% -> 5% of each run, Pallas kernels for 3% -> 0%
where the time goes in v2:
time: 53.4 us; the launch traced here: 53 us
  waiting for transfers between devices  21.9 us (41%)
  starting transfers between devices  15.6 us (29%)
  Pallas kernels  8.88 us (17%)
  other arithmetic  3.54 us (7%)
  local copies, waits for them, and re-layouts  2.35 us (4%)
  between operations  0.74 us (1%)
    ppermute x12, waiting for transfers between devices, along(): return lax.ppermute(x, axis, [(i, i ^ d) for i in range(size)])  21.9 us
    ppermute x12, starting transfers between devices, along(): return lax.ppermute(x, axis, [(i, i ^ d) for i in range(size)])  15.6 us
    pallas_call x1, Pallas kernels, on_device(): call(functools.partial(layer_kernel, ranks=ranks, local=local), [shape((t...  5.63 us
    unnamed x16, local copies, waits for them, and re-layouts  2.28 us
    pallas_call x1, Pallas kernels, on_device(): call(functools.partial(place_kernel, ranks=ranks), [grad_shape] * 3, 1, r...  1.72 us
    pallas_call x1, Pallas kernels, on_device(): call(pack_kernel, shape((local, 3 * share, block), BF16), 1, 3, [pltpu.VM...  1.53 us
    add x1, other arithmetic, on_device(): chip = near_grad.astype(F32) + over(far_grad, 1).astype(F32)  1.08 us
  transfers between devices with their start and end apart: 12, of which 10 were waited for; matrix products, arithmetic and copies ran while one was open for 5% of the time, Pallas kernels for 0%

profile of v2, /device:TPU:0, one launch (start us, length us, event | category | flops | bytes accessed | tf_op | source)
XLA Modules:
  0.0 53.0 jit_solution(4904495515273976090)
XLA Ops:
  0.6 1.5 %shard_map.111 = bf16[1,192,128]{2,1,0:T(8,128)(2,1)} custom-call(s32[1]{0:T(128)} %bitcast.1.rank_ref, bf16[1,128,128]{2,1,0:T(8,128)(2,1)} %gate_ref.1, bf16[1,128,128]{2,1,0:T(8,128)(2,1)} %up_ref.1, bf16[1,128,128]{2,1,0:T(8,128)(2,1)} %down_ref.1), custom_call_target="tpu_custom_call" | custom-call | tf_op jit(solution)/shard_map/pallas_call | solution.py:130
  2.2 5.1 %collective-permute-start.2 = (bf16[1,192,128]{2,1,0:T(8,128)(2,1)}, bf16[1,192,128]{2,1,0:T(8,128)(2,1)S(1)}, u32[]{:S(2)}, u32[]{:S(2)}) collective-permute-start(bf16[1,192,128]{2,1,0:T(8,128)(2,1)} %shard_map.111), channel_id=1, source_target_pairs={{0,24},{2,26},{4,28},{6,30},{8,16},{10,18},{12,20},{14,22},{16,8},... | collective-permute-start | bytes 147464 | tf_op jit(solution)/shard_map/ppermute | solution.py:125
  7.8 0.8 %constant_dynamic-update-slice_fusion.4 = bf16[8,192,128]{2,1,0:T(8,128)(2,1)S(1)} fusion(bf16[1,192,128]{2,1,0:T(8,128)(2,1)} %shard_map.111), kind=kLoop, calls=%fused_computation.13 | loop fusion | bytes 98304
  8.7 1.0 %collective-permute-done.2 = bf16[1,192,128]{2,1,0:T(8,128)(2,1)S(1)} collective-permute-done((bf16[1,192,128]{2,1,0:T(8,128)(2,1)}, bf16[1,192,128]{2,1,0:T(8,128)(2,1)S(1)}, u32[]{:S(2)}, u32[]{:S(2)}) %collective-permute-start.2) | collective-permute-done | bytes 49184 | tf_op jit(solution)/shard_map/ppermute | solution.py:125
  9.7 2.8 %collective-permute-done.1 = bf16[1,192,128]{2,1,0:T(8,128)(2,1)S(1)} collective-permute-done((bf16[1,192,128]{2,1,0:T(8,128)(2,1)}, bf16[1,192,128]{2,1,0:T(8,128)(2,1)S(1)}, u32[]{:S(2)}, u32[]{:S(2)}) %collective-permute-start.1) | collective-permute-done | bytes 49184 | tf_op jit(solution)/shard_map/ppermute | solution.py:125
  12.5 0.8 %pad_maximum_fusion = bf16[4,192,128]{2,1,0:T(8,128)(2,1)S(1)} fusion(bf16[1,192,128]{2,1,0:T(8,128)(2,1)S(1)} %collective-permute-done.2, bf16[1,192,128]{2,1,0:T(8,128)(2,1)S(1)} %collective-permute-done.1, bf16[1,192,128]{2,1,0:T(8,128)(2,1)S(1)} %collective-permute-done, bf16[1,192,128]{2,1,0:T(8,128)(2,1)} %shard_map.111), kind=kLoop, calls=%fused_computation.4 | loop fusion | flops 294912 | bytes 393216 | tf_op jit(solution)/shard_map/concatenate | solution.py:135
  13.3 1.6 %collective-permute-start.3 = (bf16[4,192,128]{2,1,0:T(8,128)(2,1)S(1)}, bf16[4,192,128]{2,1,0:T(8,128)(2,1)S(1)}, u32[]{:S(2)}, u32[]{:S(2)}) collective-permute-start(bf16[4,192,128]{2,1,0:T(8,128)(2,1)S(1)} %pad_maximum_fusion), channel_id=1, source_target_pairs={{0,4},{2,6},{4,0},{6,2},{8,12},{10,14},{12,8},{14,10},{16,20},{18,... | collective-permute-start | bytes 589832 | tf_op jit(solution)/shard_map/ppermute | solution.py:125
  14.9 4.2 %collective-permute-done.3 = bf16[4,192,128]{2,1,0:T(8,128)(2,1)S(1)} collective-permute-done((bf16[4,192,128]{2,1,0:T(8,128)(2,1)S(1)}, bf16[4,192,128]{2,1,0:T(8,128)(2,1)S(1)}, u32[]{:S(2)}, u32[]{:S(2)}) %collective-permute-start.3) | collective-permute-done | bytes 196640 | tf_op jit(solution)/shard_map/ppermute | solution.py:125
  19.8 1.1 %collective-permute-done.4.far_ref = bf16[8,192,128]{2,1,0:T(8,128)(2,1)S(1)} collective-permute-done((bf16[8,192,128]{2,1,0:T(8,128)(2,1)S(1)}, bf16[8,192,128]{2,1,0:T(8,128)(2,1)S(1)}, u32[]{:S(2)}, u32[]{:S(2)}) %collective-permute-start.4) | collective-permute-done | bytes 393248 | tf_op jit(solution)/shard_map/ppermute | solution.py:125
  20.9 0.8 %copy-done.3 = bf16[8,192,128]{2,1,0:T(8,128)(2,1)} copy-done((bf16[8,192,128]{2,1,0:T(8,128)(2,1)}, bf16[8,192,128]{2,1,0:T(8,128)(2,1)S(1)}, u32[]{:S(2)}) %copy-start.3) | copy-done | bytes 393240
  21.7 5.6 %shard_map.112 = (bf16[144,2048]{1,0:T(8,128)(2,1)}, bf16[144,2048]{1,0:T(8,128)(2,1)}, bf16[8,192,128]{2,1,0:T(8,128)(2,1)}, bf16[8,192,128]{2,1,0:T(8,128)(2,1)}) custom-call(s32[2]{0:T(128)} %pad_add_fusion.place_ref, s32[16]{0:T(128)} %col_ref.1, s32[16]{0:T(128)} %in_ref.1, s32[16]{0:T(128)} %out_row_ref.1, bf16[144,4096]{1,0:T(8,128)(2,1)} %tok_ref.1, ...), custom_call_target="tpu_custom_call" | custom-call | tf_op jit(solution)/shard_map/pallas_call | solution.py:140
  27.5 1.8 %collective-permute-done.6 = bf16[8,192,128]{2,1,0:T(8,128)(2,1)S(1)} collective-permute-done((bf16[8,192,128]{2,1,0:T(8,128)(2,1)}, bf16[8,192,128]{2,1,0:T(8,128)(2,1)S(1)}, u32[]{:S(2)}, u32[]{:S(2)}) %collective-permute-start.6) | collective-permute-done | bytes 393248 | tf_op jit(solution)/shard_map/ppermute | solution.py:125
  29.3 1.1 %convert_add_fusion = f32[8,192,128]{2,1,0:T(8,128)S(1)} fusion(bf16[8,192,128]{2,1,0:T(8,128)(2,1)S(1)} %collective-permute-done.6, bf16[8,192,128]{2,1,0:T(8,128)(2,1)} %get-tuple-element.13), kind=kLoop, calls=%fused_computation.1 | loop fusion | flops 589824 | bytes 1572864 | tf_op jit(solution)/shard_map/add | solution.py:158
  30.4 1.6 %collective-permute-start.7 = (bf16[4,192,128]{2,1,0:T(8,128)(2,1)S(1)}, bf16[4,192,128]{2,1,0:T(8,128)(2,1)S(1)}, u32[]{:S(2)}, u32[]{:S(2)}) collective-permute-start(bf16[4,192,128]{2,1,0:T(8,128)(2,1)S(1)} %slice.43), channel_id=1, source_target_pairs={{0,4},{2,6},{4,0},{6,2},{8,12},{10,14},{12,8},{14,10},{16,20},{18,... | collective-permute-start | bytes 589832 | tf_op jit(solution)/shard_map/ppermute | solution.py:125
  32.0 1.5 %collective-permute-start.5 = (bf16[144,2048]{1,0:T(8,128)(2,1)S(1)}, bf16[144,2048]{1,0:T(8,128)(2,1)S(1)}, u32[]{:S(2)}, u32[]{:S(2)}) collective-permute-start(bf16[144,2048]{1,0:T(8,128)(2,1)S(1)} %copy-done.5), channel_id=1, source_target_pairs={{0,1},{1,0},{2,3},{3,2},{4,5},{5,4},{6,7},{7,6},{8,9},{9,8},{10,11... | collective-permute-start | bytes 1769480 | tf_op jit(solution)/shard_map/ppermute | solution.py:125
  33.5 3.9 %collective-permute-done.7 = bf16[4,192,128]{2,1,0:T(8,128)(2,1)S(1)} collective-permute-done((bf16[4,192,128]{2,1,0:T(8,128)(2,1)S(1)}, bf16[4,192,128]{2,1,0:T(8,128)(2,1)S(1)}, u32[]{:S(2)}, u32[]{:S(2)}) %collective-permute-start.7) | collective-permute-done | bytes 196640 | tf_op jit(solution)/shard_map/ppermute | solution.py:125
  37.5 0.8 %collective-permute-start.8 = (bf16[1,192,128]{2,1,0:T(8,128)(2,1)S(1)}, bf16[1,192,128]{2,1,0:T(8,128)(2,1)S(1)}, u32[]{:S(2)}, u32[]{:S(2)}) collective-permute-start(bf16[1,192,128]{2,1,0:T(8,128)(2,1)S(1)} %get-tuple-element.20), channel_id=1, source_target_pairs={{0,8},{2,10},{4,12},{6,14},{8,0},{10,2},{12,4},{14,6},{16,24},{18,... | collective-permute-start | bytes 147464 | tf_op jit(solution)/shard_map/ppermute | solution.py:125
  38.3 2.7 %collective-permute-start.10 = (bf16[1,192,128]{2,1,0:T(8,128)(2,1)S(1)}, bf16[1,192,128]{2,1,0:T(8,128)(2,1)S(1)}, u32[]{:S(2)}, u32[]{:S(2)}) collective-permute-start(bf16[1,192,128]{2,1,0:T(8,128)(2,1)S(1)} %get-tuple-element.21), channel_id=1, source_target_pairs={{0,24},{2,26},{4,28},{6,30},{8,16},{10,18},{12,20},{14,22},{16,8},... | collective-permute-start | bytes 147464 | tf_op jit(solution)/shard_map/ppermute | solution.py:125
  41.6 2.6 %collective-permute-done.10 = bf16[1,192,128]{2,1,0:T(8,128)(2,1)S(1)} collective-permute-done((bf16[1,192,128]{2,1,0:T(8,128)(2,1)S(1)}, bf16[1,192,128]{2,1,0:T(8,128)(2,1)S(1)}, u32[]{:S(2)}, u32[]{:S(2)}) %collective-permute-start.10) | collective-permute-done | bytes 49184 | tf_op jit(solution)/shard_map/ppermute | solution.py:125
  44.3 1.7 %collective-permute-done.9 = bf16[1,192,128]{2,1,0:T(8,128)(2,1)S(1)} collective-permute-done((bf16[1,192,128]{2,1,0:T(8,128)(2,1)S(1)}, bf16[1,192,128]{2,1,0:T(8,128)(2,1)S(1)}, u32[]{:S(2)}, u32[]{:S(2)}) %collective-permute-start.9) | collective-permute-done | bytes 49184 | tf_op jit(solution)/shard_map/ppermute | solution.py:125
  46.0 1.6 %collective-permute-start.11 = (f32[1,192,128]{2,1,0:T(8,128)S(1)}, f32[1,192,128]{2,1,0:T(8,128)S(1)}, u32[]{:S(2)}, u32[]{:S(2)}) collective-permute-start(f32[1,192,128]{2,1,0:T(8,128)S(1)} %fusion.2.refs_0_), channel_id=1, source_target_pairs={{0,1},{1,0},{2,3},{3,2},{4,5},{5,4},{6,7},{7,6},{8,9},{9,8},{10,11... | collective-permute-start | bytes 294920 | tf_op jit(solution)/shard_map/ppermute | solution.py:125
  47.6 1.0 %add_convert_fusion = bf16[144,2048]{1,0:T(8,128)(2,1)} fusion(bf16[144,2048]{1,0:T(8,128)(2,1)S(1)} %collective-permute-done.5, bf16[144,2048]{1,0:T(8,128)(2,1)S(1)} %copy-done), kind=kLoop, calls=%fused_computation | loop fusion | flops 1179648 | bytes 1769472 | tf_op jit(solution)/shard_map/convert_element_type | solution.py:177
  48.5 2.1 %collective-permute-done.11.refs_1_ = f32[1,192,128]{2,1,0:T(8,128)S(1)} collective-permute-done((f32[1,192,128]{2,1,0:T(8,128)S(1)}, f32[1,192,128]{2,1,0:T(8,128)S(1)}, u32[]{:S(2)}, u32[]{:S(2)}) %collective-permute-start.11) | collective-permute-done | bytes 98336 | tf_op jit(solution)/shard_map/ppermute | solution.py:125
  51.3 1.7 %shard_map.113 = (f32[1,128,128]{2,1,0:T(8,128)}, f32[1,128,128]{2,1,0:T(8,128)}, f32[1,128,128]{2,1,0:T(8,128)}) custom-call(s32[1]{0:T(128)} %bitcast.1.rank_ref, f32[1,192,128]{2,1,0:T(8,128)} %copy-done.2, f32[1,192,128]{2,1,0:T(8,128)} %copy-done.4), custom_call_target="tpu_custom_call" | custom-call | tf_op jit(solution)/shard_map/pallas_call | solution.py:167
  (28 shorter events, 2.9 us)
Async XLA Ops:
  2.2 7.5 %collective-permute-start.2 = (bf16[1,192,128]{2,1,0:T(8,128)(2,1)}, bf16[1,192,128]{2,1,0:T(8,128)(2,1)S(1)}, u32[]{:S(2)}, u32[]{:S(2)}) collective-permute-start(bf16[1,192,128]{2,1,0:T(8,128)(2,1)} %shard_map.111), channel_id=1, source_target_pairs={{0,24},{2,26},{4,28},{6,30},{8,16},{10,18},{12,20},{14,22},{16,8},... | collective-permute-start | bytes 147464 | tf_op jit(solution)/shard_map/ppermute | solution.py:125
  7.2 5.2 %collective-permute-start.1 = (bf16[1,192,128]{2,1,0:T(8,128)(2,1)}, bf16[1,192,128]{2,1,0:T(8,128)(2,1)S(1)}, u32[]{:S(2)}, u32[]{:S(2)}) collective-permute-start(bf16[1,192,128]{2,1,0:T(8,128)(2,1)} %shard_map.111), channel_id=1, source_target_pairs={{0,16},{2,18},{4,20},{6,22},{8,24},{10,26},{12,28},{14,30},{16,0},... | collective-permute-start | bytes 147464 | tf_op jit(solution)/shard_map/ppermute | solution.py:125
  7.3 5.2 %collective-permute-start = (bf16[1,192,128]{2,1,0:T(8,128)(2,1)}, bf16[1,192,128]{2,1,0:T(8,128)(2,1)S(1)}, u32[]{:S(2)}, u32[]{:S(2)}) collective-permute-start(bf16[1,192,128]{2,1,0:T(8,128)(2,1)} %shard_map.111), channel_id=1, source_target_pairs={{0,8},{2,10},{4,12},{6,14},{8,0},{10,2},{12,4},{14,6},{16,24},{18,... | collective-permute-start | bytes 147464 | tf_op jit(solution)/shard_map/ppermute | solution.py:125
  13.3 5.8 %collective-permute-start.3 = (bf16[4,192,128]{2,1,0:T(8,128)(2,1)S(1)}, bf16[4,192,128]{2,1,0:T(8,128)(2,1)S(1)}, u32[]{:S(2)}, u32[]{:S(2)}) collective-permute-start(bf16[4,192,128]{2,1,0:T(8,128)(2,1)S(1)} %pad_maximum_fusion), channel_id=1, source_target_pairs={{0,4},{2,6},{4,0},{6,2},{8,12},{10,14},{12,8},{14,10},{16,20},{18,... | collective-permute-start | bytes 589832 | tf_op jit(solution)/shard_map/ppermute | solution.py:125
  19.1 1.8 %copy-start.1 = (bf16[8,192,128]{2,1,0:T(8,128)(2,1)}, bf16[8,192,128]{2,1,0:T(8,128)(2,1)S(1)}, u32[]{:S(2)}) copy-start(bf16[8,192,128]{2,1,0:T(8,128)(2,1)S(1)} %constant_dynamic-update-slice_fusion.near_ref) | copy-start | bytes 1179652
  19.1 1.8 %collective-permute-start.4 = (bf16[8,192,128]{2,1,0:T(8,128)(2,1)S(1)}, bf16[8,192,128]{2,1,0:T(8,128)(2,1)S(1)}, u32[]{:S(2)}, u32[]{:S(2)}) collective-permute-start(bf16[8,192,128]{2,1,0:T(8,128)(2,1)S(1)} %constant_dynamic-update-slice_fusion.near_ref), channel_id=1, source_target_pairs={{0,2},{2,0},{4,6},{6,4},{8,10},{10,8},{12,14},{14,12},{16,18},{18,... | collective-permute-start | bytes 1179656 | tf_op jit(solution)/shard_map/ppermute | solution.py:125
  20.9 0.8 %copy-start.3 = (bf16[8,192,128]{2,1,0:T(8,128)(2,1)}, bf16[8,192,128]{2,1,0:T(8,128)(2,1)S(1)}, u32[]{:S(2)}) copy-start(bf16[8,192,128]{2,1,0:T(8,128)(2,1)S(1)} %collective-permute-done.4.far_ref) | copy-start | bytes 1179652
  27.3 4.7 %copy-start.5 = (bf16[144,2048]{1,0:T(8,128)(2,1)S(1)}, bf16[144,2048]{1,0:T(8,128)(2,1)}, u32[]{:S(2)}) copy-start(bf16[144,2048]{1,0:T(8,128)(2,1)} %get-tuple-element.12) | copy-start | bytes 1769476
  27.3 1.9 %collective-permute-start.6 = (bf16[8,192,128]{2,1,0:T(8,128)(2,1)}, bf16[8,192,128]{2,1,0:T(8,128)(2,1)S(1)}, u32[]{:S(2)}, u32[]{:S(2)}) collective-permute-start(bf16[8,192,128]{2,1,0:T(8,128)(2,1)} %get-tuple-element.14), channel_id=1, source_target_pairs={{0,2},{2,0},{4,6},{6,4},{8,10},{10,8},{12,14},{14,12},{16,18},{18,... | collective-permute-start | bytes 1179656 | tf_op jit(solution)/shard_map/ppermute | solution.py:125
  30.3 17.2 %copy-start = (bf16[144,2048]{1,0:T(8,128)(2,1)S(1)}, bf16[144,2048]{1,0:T(8,128)(2,1)}, u32[]{:S(2)}) copy-start(bf16[144,2048]{1,0:T(8,128)(2,1)} %get-tuple-element.11) | copy-start | bytes 1769476
  30.4 7.0 %collective-permute-start.7 = (bf16[4,192,128]{2,1,0:T(8,128)(2,1)S(1)}, bf16[4,192,128]{2,1,0:T(8,128)(2,1)S(1)}, u32[]{:S(2)}, u32[]{:S(2)}) collective-permute-start(bf16[4,192,128]{2,1,0:T(8,128)(2,1)S(1)} %slice.43), channel_id=1, source_target_pairs={{0,4},{2,6},{4,0},{6,2},{8,12},{10,14},{12,8},{14,10},{16,20},{18,... | collective-permute-start | bytes 589832 | tf_op jit(solution)/shard_map/ppermute | solution.py:125
  32.0 15.6 %collective-permute-start.5 = (bf16[144,2048]{1,0:T(8,128)(2,1)S(1)}, bf16[144,2048]{1,0:T(8,128)(2,1)S(1)}, u32[]{:S(2)}, u32[]{:S(2)}) collective-permute-start(bf16[144,2048]{1,0:T(8,128)(2,1)S(1)} %copy-done.5), channel_id=1, source_target_pairs={{0,1},{1,0},{2,3},{3,2},{4,5},{5,4},{6,7},{7,6},{8,9},{9,8},{10,11... | collective-permute-start | bytes 1769480 | tf_op jit(solution)/shard_map/ppermute | solution.py:125
  37.5 4.2 %collective-permute-start.8 = (bf16[1,192,128]{2,1,0:T(8,128)(2,1)S(1)}, bf16[1,192,128]{2,1,0:T(8,128)(2,1)S(1)}, u32[]{:S(2)}, u32[]{:S(2)}) collective-permute-start(bf16[1,192,128]{2,1,0:T(8,128)(2,1)S(1)} %get-tuple-element.20), channel_id=1, source_target_pairs={{0,8},{2,10},{4,12},{6,14},{8,0},{10,2},{12,4},{14,6},{16,24},{18,... | collective-permute-start | bytes 147464 | tf_op jit(solution)/shard_map/ppermute | solution.py:125
  38.3 6.0 %collective-permute-start.10 = (bf16[1,192,128]{2,1,0:T(8,128)(2,1)S(1)}, bf16[1,192,128]{2,1,0:T(8,128)(2,1)S(1)}, u32[]{:S(2)}, u32[]{:S(2)}) collective-permute-start(bf16[1,192,128]{2,1,0:T(8,128)(2,1)S(1)} %get-tuple-element.21), channel_id=1, source_target_pairs={{0,24},{2,26},{4,28},{6,30},{8,16},{10,18},{12,20},{14,22},{16,8},... | collective-permute-start | bytes 147464 | tf_op jit(solution)/shard_map/ppermute | solution.py:125
  41.0 5.0 %collective-permute-start.9 = (bf16[1,192,128]{2,1,0:T(8,128)(2,1)S(1)}, bf16[1,192,128]{2,1,0:T(8,128)(2,1)S(1)}, u32[]{:S(2)}, u32[]{:S(2)}) collective-permute-start(bf16[1,192,128]{2,1,0:T(8,128)(2,1)S(1)} %get-tuple-element.22), channel_id=1, source_target_pairs={{0,16},{2,18},{4,20},{6,22},{8,24},{10,26},{12,28},{14,30},{16,0},... | collective-permute-start | bytes 147464 | tf_op jit(solution)/shard_map/ppermute | solution.py:125
  46.0 4.7 %copy-start.2 = (f32[1,192,128]{2,1,0:T(8,128)}, f32[1,192,128]{2,1,0:T(8,128)S(1)}, u32[]{:S(2)}) copy-start(f32[1,192,128]{2,1,0:T(8,128)S(1)} %fusion.2.refs_0_) | copy-start | bytes 294916
  46.0 4.7 %collective-permute-start.11 = (f32[1,192,128]{2,1,0:T(8,128)S(1)}, f32[1,192,128]{2,1,0:T(8,128)S(1)}, u32[]{:S(2)}, u32[]{:S(2)}) collective-permute-start(f32[1,192,128]{2,1,0:T(8,128)S(1)} %fusion.2.refs_0_), channel_id=1, source_target_pairs={{0,1},{1,0},{2,3},{3,2},{4,5},{5,4},{6,7},{7,6},{8,9},{9,8},{10,11... | collective-permute-start | bytes 294920 | tf_op jit(solution)/shard_map/ppermute | solution.py:125
  50.7 0.6 %copy-start.4 = (f32[1,192,128]{2,1,0:T(8,128)}, f32[1,192,128]{2,1,0:T(8,128)S(1)}, u32[]{:S(2)}) copy-start(f32[1,192,128]{2,1,0:T(8,128)S(1)} %collective-permute-done.11.refs_1_) | copy-start | bytes 294916

commit v3 on v2

v3 whole, which is shorter than its diff:
```python
import functools

import jax
import jax.numpy as jnp
from jax import lax
from jax.experimental import pallas as pl
from jax.experimental.pallas import tpu as pltpu
from jax.sharding import PartitionSpec as P

VMEM = pltpu.MemorySpace.VMEM
SMEM = pltpu.MemorySpace.SMEM
HBM = pltpu.MemorySpace.HBM
F32 = jnp.float32
BF16 = jnp.bfloat16


def dot(a, b, dim_a, dim_b):
    return lax.dot_general(a, b, (((dim_a,), (dim_b,)), ((), ())), preferred_element_type=F32)


def pack_kernel(rank_ref, gate_ref, up_ref, down_ref, out_ref, held, turned, sems):
    share = out_ref.shape[1] // 3
    first = pl.multiple_of(rank_ref[0] * share, share)
    copies = [
        pltpu.make_async_copy(ref, held.at[part], sems.at[part])
        for part, ref in enumerate((gate_ref, up_ref, down_ref))
    ]
    for copy in copies:
        copy.start()
    for part, copy in enumerate(copies):
        copy.wait()
        for i in range(out_ref.shape[0]):
            whole = held[part, i].astype(F32)
            turned[...] = whole if part == 2 else whole.T
            out_ref[i, part * share : (part + 1) * share] = turned[pl.ds(first, share), :].astype(BF16)


class Slots:
    def __init__(self, me, count, local):
        self.count, self.half, self.quarter = count, count // 2, count // 4
        self.keys = []
        for slot in range(count):
            at, inner = slot // local, slot % local
            fars = self.quarter // local
            side, pair, far = at // (2 * fars), (at // fars) % 2, at % fars
            self.keys.append((me ^ (far * 4 + pair * 2 + side)) * local + inner)

    def heads(self, col_ref):
        cols = [col_ref[key] for key in self.keys]
        found = []
        for slot in range(self.count):
            best = jnp.int32(slot)
            for earlier in reversed(range(slot)):
                best = jnp.where(cols[earlier] == cols[slot], earlier, best)
            found.append(best)
        return found


def forward(w_ref, at, tok, cot, gu_ref, dh_ref, to):
    two = gu_ref.shape[1]
    gu_ref[to] = dot(w_ref[at, :two], tok, 1, 1)
    dh_ref[to] = dot(w_ref[at, two:], cot, 1, 1)


def backward(grad_ref, at, gu_grad, hidden, tok, cot):
    two = gu_grad.shape[0]
    grad_ref[at, :two] = dot(gu_grad, tok, 1, 0).astype(BF16)
    grad_ref[at, two:] = dot(hidden, cot, 1, 0).astype(BF16)


def first_kernel(me_ref, in_ref, out_row_ref, tokens, cotangent, w_ref, tok_ref, cot_ref, gu_ref, dh_ref, sems, *, local):
    count, _, block = tok_ref.shape
    slots = Slots(me_ref[0], count, local)

    def column(array, index):
        return array.at[:, pl.ds(pl.multiple_of(index * block, block), block)]

    copies = []
    for slot, key in enumerate(slots.keys):
        copies.append(
            (
                pltpu.make_async_copy(column(tokens, in_ref[key]), tok_ref.at[slot], sems.at[0, slot]),
                pltpu.make_async_copy(column(cotangent, out_row_ref[key]), cot_ref.at[slot], sems.at[1, slot]),
            )
        )
        for copy in copies[-1]:
            copy.start()
    for pair in copies:
        for copy in pair:
            copy.wait()
    for slot in range(slots.quarter):
        forward(w_ref, slot, tok_ref[slot], cot_ref[slot], gu_ref, dh_ref, slot)


def second_kernel(w_ref, tok_ref, cot_ref, gu_ref, dh_ref):
    quarter = w_ref.shape[0]
    for slot in range(quarter):
        forward(w_ref, slot, tok_ref[quarter + slot], cot_ref[quarter + slot], gu_ref, dh_ref, slot)


def third_kernel(
    me_ref, col_ref, w_ref, tok_ref, cot_ref, gu0, gu1, dh0, dh1, grad_ref, gu_grad, hidden, gu, dh, *, local
):
    count, two, _ = gu_grad.shape
    share = two // 2
    slots = Slots(me_ref[0], count, local)
    heads = slots.heads(col_ref)
    half, quarter = slots.half, slots.quarter
    for slot in range(quarter):
        gu[slot], gu[quarter + slot] = gu0[slot], gu1[slot]
        dh[slot], dh[quarter + slot] = dh0[slot], dh1[slot]
    for slot in range(half, count):
        forward(w_ref, slot - half, tok_ref[slot], cot_ref[slot], gu, dh, slot)
    for slot in range(1, count):

        @pl.when(heads[slot] != slot)
        def _(slot=slot):
            gu[heads[slot]] += gu[slot]
            dh[heads[slot]] += dh[slot]

    for slot in range(count):
        gate, up, grad = gu[slot, :share], gu[slot, share:], dh[slot]
        sig = jax.nn.sigmoid(gate)
        act = gate * sig
        hidden[slot] = (act * up).astype(BF16)
        gu_grad[slot, :share] = (grad * up * sig * (1.0 + gate * (1.0 - sig))).astype(BF16)
        gu_grad[slot, share:] = (grad * act).astype(BF16)
    for slot in range(half, count):
        head = heads[slot]
        backward(grad_ref, slot - half, gu_grad[head], hidden[head], tok_ref[slot], cot_ref[slot])


def fourth_kernel(
    me_ref, rank_ref, col_ref, in_ref, near_ref, far_ref, tok_ref, cot_ref, gu_grad, hidden, *rest, ranks, local
):
    spread_refs, (grad_ref, total) = rest[:ranks], rest[ranks:]
    count, two, _ = gu_grad.shape
    block = tok_ref.shape[2]
    slots = Slots(me_ref[0], count, local)
    heads = slots.heads(col_ref)
    half = slots.half
    total[...] = jnp.zeros_like(total)
    for slot in range(count):
        weight = near_ref[slot, :two] if slot < half else far_ref[slot - half, :two]
        total[in_ref[slots.keys[slot]]] += dot(gu_grad[heads[slot]], weight, 0, 0)
    per = total.shape[0] // ranks
    for d in range(ranks):
        for r in range(per):
            spread_refs[d][:, r * block : (r + 1) * block] = total[(rank_ref[0] ^ d) * per + r].astype(BF16)
    for slot in range(half):
        head = heads[slot]
        backward(grad_ref, slot, gu_grad[head], hidden[head], tok_ref[slot], cot_ref[slot])


def place_kernel(rank_ref, *refs, ranks):
    pieces, (gate_ref, up_ref, down_ref, whole) = refs[:ranks], refs[ranks:]
    share = pieces[0].shape[1] // 3
    for i in range(gate_ref.shape[0]):
        for part, ref in enumerate((gate_ref, up_ref, down_ref)):
            for d in range(ranks):
                at = pl.multiple_of((rank_ref[0] ^ d) * share, share)
                whole[pl.ds(at, share), :] = pieces[d][i, part * share : (part + 1) * share].astype(F32)
            ref[i] = whole[...] if part == 2 else whole[...].T


def call(kernel, out_shape, spaces, scratch=(), mib=4, flops=0):
    where = {"s": SMEM, "h": HBM, "v": VMEM}
    return pl.pallas_call(
        kernel,
        out_shape=out_shape,
        in_specs=[pl.BlockSpec(memory_space=where[c]) for c in spaces],
        out_specs=jax.tree.map(lambda _: pl.BlockSpec(memory_space=VMEM), out_shape),
        scratch_shapes=list(scratch),
        compiler_params=pltpu.CompilerParams(vmem_limit_bytes=mib << 20),
        cost_estimate=pl.CostEstimate(flops=flops, bytes_accessed=flops // 256, transcendentals=0) if flops else None,
    )


def outside(x):
    return pltpu.with_memory_space_constraint(x, HBM)


def on_device(tokens, cotangent, gate_blocks, up_blocks, down_blocks, col_block, in_row, out_row):
    token_count, width = tokens.shape
    local, block, _ = gate_blocks.shape
    count = col_block.shape[0]
    groups, ranks = lax.axis_size("dp"), lax.axis_size("mp")
    share = block // ranks
    two, rows = 2 * share, 3 * share
    fars = groups // 4
    quarter = fars * local
    me = lax.axis_index("dp").astype(jnp.int32).reshape(1)
    rank = lax.axis_index("mp").astype(jnp.int32).reshape(1)
    scale = (token_count * groups) ** -0.5
    macs = 2 * token_count * block * rows

    def f32(*dims):
        return jax.ShapeDtypeStruct(dims, F32)

    def bf16(*dims):
        return jax.ShapeDtypeStruct(dims, BF16)

    def along(x, axis, size, d):
        return lax.ppermute(x, axis, [(i, i ^ d) for i in range(size)])

    def over(x, d):
        return along(x, "dp", groups, d)

    def across(x, d):
        return along(x, "mp", ranks, d)

    own = call(
        pack_kernel,
        bf16(local, rows, block),
        "shhh",
        [
            pltpu.VMEM((3, local, block, block), BF16),
            pltpu.VMEM((block, block), F32),
            pltpu.SemaphoreType.DMA((3,)),
        ],
    )(rank, *map(outside, (gate_blocks, up_blocks, down_blocks)))
    column = jnp.concatenate([own] + [over(own, 4 * i) for i in range(1, fars)], axis=0)
    beside = over(column, 2)
    some_gu, some_dh = f32(quarter, two, token_count), f32(quarter, share, token_count)
    tok, cot, gu0, dh0 = call(
        functools.partial(first_kernel, local=local),
        [bf16(count, token_count, block)] * 2 + [some_gu, some_dh],
        "ssshhv",
        [pltpu.SemaphoreType.DMA((2, count))],
        8,
        macs * quarter,
    )(me, in_row, out_row, outside(tokens), outside(cotangent), column)
    beside, tok = lax.optimization_barrier((beside, tok))
    near = jnp.concatenate([column, beside], axis=0)
    far = over(near, 1)
    gu1, dh1 = call(second_kernel, [some_gu, some_dh], "vvv", (), 8, macs * quarter)(beside, tok, cot)
    grad_parts = bf16(2 * quarter, rows, block)
    far_grad, gu_grad, hidden = call(
        functools.partial(third_kernel, local=local),
        [grad_parts, bf16(count, two, token_count), bf16(count, share, token_count)],
        "ssvvvvvvv",
        [pltpu.VMEM((count, two, token_count), F32), pltpu.VMEM((count, share, token_count), F32)],
        12,
        macs * count,
    )(me, col_block, far, tok, cot, gu0, gu1, dh0, dh1)
    *spread, near_grad = call(
        functools.partial(fourth_kernel, ranks=ranks, local=local),
        [bf16(token_count, width // ranks)] * ranks + [grad_parts],
        "ssssvvvvvv",
        [pltpu.VMEM((width // block, token_count, block), F32)],
        12,
        macs * count,
    )(me, rank, col_block, in_row, near, far, tok, cot, gu_grad, hidden)

    arrived = [across(spread[d], d) for d in range(1, ranks)]
    chip = near_grad.astype(F32) + over(far_grad, 1).astype(F32)
    plane = chip[:quarter] + over(chip[quarter:].astype(BF16), 2).astype(F32)
    summed = plane[:local]
    for i in range(1, fars):
        piece = plane[i * local : (i + 1) * local].astype(BF16)
        summed = summed + over(piece, 4 * i).astype(F32)
    summed = summed * scale
    pieces = [summed] + [across(summed.astype(BF16), d) for d in range(1, ranks)]
    gate_grads, up_grads, down_grads = call(
        functools.partial(place_kernel, ranks=ranks),
        [f32(local, block, block)] * 3,
        "s" + "v" * ranks,
        [pltpu.VMEM((block, block), F32)],
    )(rank, *pieces)
    input_grad = spread[0].astype(F32)
    for piece in arrived:
        input_grad = input_grad + piece.astype(F32)
    return input_grad.astype(BF16), gate_grads, up_grads, down_grads


def solution(mesh):
    flat = P("dp", None, None)
    return jax.shard_map(
        on_device,
        mesh=mesh,
        in_specs=(P("dp", None), P("dp", None), flat, flat, flat, P(), P(), P()),
        out_specs=(P("dp", "mp"), flat, flat, flat),
        check_vma=False,
    )
```

time: 53.4 us -> 44.7 us (0.84)
  waiting for transfers between devices: 21.9 us -> 16.8 us
  other arithmetic: 3.54 us -> 1.16 us
  local copies, waits for them, and re-layouts: 2.35 us -> 1.43 us
    ppermute x12, waiting for transfers between devices: 21.9 us -> 16.8 us  [along(): return lax.ppermute(x, axis, [(i, i ^ d) for i in range(size)])]
    add x1, other arithmetic: 1.08 us -> 0.08 us  [on_device(): chip = near_grad.astype(F32) + over(far_grad, 1).astype(F32)]
    unnamed x16 -> x12, local copies, waits for them, and re-layouts: 2.28 us -> 1.36 us
    concatenate x1, other arithmetic: 0.83 us -> 0.03 us  [on_device(): jnp.concatenate([own] + [over(own, 4 * i) for i in range(1, fars)], axis=0)]
    concatenate x1 -> x0, other arithmetic: 0.59 us -> none  [on_device(): jnp.concatenate([lax.axis_index('dp').astype(jnp.int32).reshape(1), rank])]
    pallas_call x3 -> x6, Pallas kernels: 8.88 us -> 8.4 us  [the longest x1 2.47 us: on_device(): call(functools.partial(first_kernel, local=local), [bf16(count, token_cou...]
  transfers between devices with their start and end apart: 12 -> 12, of which waited for: 10 -> 9; matrix products, arithmetic and copies ran while one was open for 5% -> 2% of each run, Pallas kernels for 0% -> 10%
where the time goes in v3:
time: 44.7 us; the launch traced here: 44.4 us
  waiting for transfers between devices  16.8 us (38%)
  starting transfers between devices  15.8 us (35%)
  Pallas kernels  8.4 us (19%)
  local copies, waits for them, and re-layouts  1.43 us (3%)
  other arithmetic  1.16 us (3%)
  between operations  0.76 us (2%)
    ppermute x12, waiting for transfers between devices, along(): return lax.ppermute(x, axis, [(i, i ^ d) for i in range(size)])  16.8 us
    ppermute x12, starting transfers between devices, along(): return lax.ppermute(x, axis, [(i, i ^ d) for i in range(size)])  15.8 us
    pallas_call x1, Pallas kernels, on_device(): call(functools.partial(first_kernel, local=local), [bf16(count, token_cou...  2.47 us
    pallas_call x1, Pallas kernels, on_device(): call(functools.partial(third_kernel, local=local), [grad_parts, bf16(coun...  2.17 us
    pallas_call x1, Pallas kernels, on_device(): call(functools.partial(fourth_kernel, ranks=ranks, local=local), [bf16(to...  1.65 us
    unnamed x12, local copies, waits for them, and re-layouts  1.36 us
    pallas_call x1, Pallas kernels, on_device(): call(pack_kernel, bf16(local, rows, block), 'shhh', [pltpu.VMEM((3, local...  1.01 us
    convert_element_type x1, other arithmetic, on_device(): return (input_grad.astype(BF16), gate_grads, up_grads, down_grads)  0.97 us
  transfers between devices with their start and end apart: 12, of which 9 were waited for; matrix products, arithmetic and copies ran while one was open for 2% of the time, Pallas kernels for 10%

profile of v3, /device:TPU:0, one launch (start us, length us, event | category | flops | bytes accessed | tf_op | source)
XLA Modules:
  0.0 44.4 jit_solution(14741980931439529301)
XLA Ops:
  0.6 1.0 %shard_map.111 = bf16[1,192,128]{2,1,0:T(8,128)(2,1)S(1)} custom-call(s32[1]{0:T(128)} %bitcast.1.rank_ref, bf16[1,128,128]{2,1,0:T(8,128)(2,1)} %gate_ref.1, bf16[1,128,128]{2,1,0:T(8,128)(2,1)} %up_ref.1, bf16[1,128,128]{2,1,0:T(8,128)(2,1)} %down_ref.1), custom_call_target="tpu_custom_call" | custom-call | tf_op jit(solution)/shard_map/pallas_call | solution.py:212
  1.7 5.1 %collective-permute-start.2 = (bf16[1,192,128]{2,1,0:T(8,128)(2,1)S(1)}, bf16[1,192,128]{2,1,0:T(8,128)(2,1)S(1)}, u32[]{:S(2)}, u32[]{:S(2)}) collective-permute-start(bf16[1,192,128]{2,1,0:T(8,128)(2,1)S(1)} %shard_map.111), channel_id=1, source_target_pairs={{0,24},{2,26},{4,28},{6,30},{8,16},{10,18},{12,20},{14,22},{16,8},... | collective-permute-start | bytes 147464 | tf_op jit(solution)/shard_map/ppermute | solution.py:204
  6.8 0.6 %collective-permute-start = (bf16[1,192,128]{2,1,0:T(8,128)(2,1)S(1)}, bf16[1,192,128]{2,1,0:T(8,128)(2,1)S(1)}, u32[]{:S(2)}, u32[]{:S(2)}) collective-permute-start(bf16[1,192,128]{2,1,0:T(8,128)(2,1)S(1)} %shard_map.111), channel_id=1, source_target_pairs={{0,8},{2,10},{4,12},{6,14},{8,0},{10,2},{12,4},{14,6},{16,24},{18,... | collective-permute-start | bytes 147464 | tf_op jit(solution)/shard_map/ppermute | solution.py:204
  7.4 1.5 %collective-permute-done.2 = bf16[1,192,128]{2,1,0:T(8,128)(2,1)S(1)} collective-permute-done((bf16[1,192,128]{2,1,0:T(8,128)(2,1)S(1)}, bf16[1,192,128]{2,1,0:T(8,128)(2,1)S(1)}, u32[]{:S(2)}, u32[]{:S(2)}) %collective-permute-start.2) | collective-permute-done | bytes 49184 | tf_op jit(solution)/shard_map/ppermute | solution.py:204
  8.9 2.9 %collective-permute-done.1 = bf16[1,192,128]{2,1,0:T(8,128)(2,1)S(1)} collective-permute-done((bf16[1,192,128]{2,1,0:T(8,128)(2,1)S(1)}, bf16[1,192,128]{2,1,0:T(8,128)(2,1)S(1)}, u32[]{:S(2)}, u32[]{:S(2)}) %collective-permute-start.1) | collective-permute-done | bytes 49184 | tf_op jit(solution)/shard_map/ppermute | solution.py:204
  11.8 1.6 %collective-permute-start.3 = (bf16[4,192,128]{2,1,0:T(8,128)(2,1)S(1)}, bf16[4,192,128]{2,1,0:T(8,128)(2,1)S(1)}, u32[]{:S(2)}, u32[]{:S(2)}) collective-permute-start(bf16[4,192,128]{2,1,0:T(8,128)(2,1)S(1)} %pad_maximum_fusion.w_ref), channel_id=1, source_target_pairs={{0,4},{2,6},{4,0},{6,2},{8,12},{10,14},{12,8},{14,10},{16,20},{18,... | collective-permute-start | bytes 589832 | tf_op jit(solution)/shard_map/ppermute | solution.py:204
  13.4 0.7 %copy-done.1 = s32[16]{0:T(128)S(1)} copy-done((s32[16]{0:T(128)S(1)}, s32[16]{0:T(128)}, u32[]{:S(2)}) %copy-start.1) | copy-done | bytes 88
  14.1 0.7 %copy-done.3 = s32[16]{0:T(128)S(1)} copy-done((s32[16]{0:T(128)S(1)}, s32[16]{0:T(128)}, u32[]{:S(2)}) %copy-start.3) | copy-done | bytes 88
  14.7 2.5 %shard_map.112 = (bf16[16,144,128]{2,1,0:T(8,128)(2,1)S(1)}, bf16[16,144,128]{2,1,0:T(8,128)(2,1)S(1)}, f32[4,128,144]{2,1,0:T(8,128)S(1)}, f32[4,64,144]{2,1,0:T(8,128)S(1)}) custom-call(s32[1]{0:T(128)} %bitcast.me_ref, s32[16]{0:T(128)S(1)} %copy-done.1, s32[16]{0:T(128)S(1)} %copy-done.3, bf16[144,4096]{1,0:T(8,128)(2,1)} %tokens.1, ...), custom_call_target="tpu_custom_call" | custom-call | flops 28311552 | bytes 110592 | tf_op jit(solution)/shard_map/pallas_call | solution.py:225
  18.1 1.4 %collective-permute-done.4.w_ref.far_ref = bf16[8,192,128]{2,1,0:T(8,128)(2,1)S(1)} collective-permute-done((bf16[8,192,128]{2,1,0:T(8,128)(2,1)S(1)}, bf16[8,192,128]{2,1,0:T(8,128)(2,1)S(1)}, u32[]{:S(2)}, u32[]{:S(2)}) %collective-permute-start.4) | collective-permute-done | bytes 393248 | tf_op jit(solution)/shard_map/ppermute | solution.py:204
  19.5 2.2 %shard_map.114 = (bf16[8,192,128]{2,1,0:T(8,128)(2,1)S(1)}, bf16[16,128,144]{2,1,0:T(8,128)(2,1)S(1)}, bf16[16,64,144]{2,1,0:T(8,128)(2,1)S(1)}) custom-call(s32[1]{0:T(128)} %bitcast.me_ref, s32[16]{0:T(128)S(1)} %copy-done, bf16[8,192,128]{2,1,0:T(8,128)(2,1)S(1)} %collective-permute-done.4.w_ref.far_ref, ...), custom_call_target="tpu_custom_call" | custom-call | flops 113246208 | bytes 442368 | tf_op jit(solution)/shard_map/pallas_call | solution.py:238
  21.8 1.6 %shard_map.115 = (bf16[144,2048]{1,0:T(8,128)(2,1)S(1)}, bf16[144,2048]{1,0:T(8,128)(2,1)S(1)}, bf16[8,192,128]{2,1,0:T(8,128)(2,1)S(1)}) custom-call(s32[1]{0:T(128)} %bitcast.me_ref, s32[1]{0:T(128)} %bitcast.1.rank_ref, s32[16]{0:T(128)S(1)} %copy-done, s32[16]{0:T(128)S(1)} %copy-done.2, ...), custom_call_target="tpu_custom_call" | custom-call | flops 113246208 | bytes 442368 | tf_op jit(solution)/shard_map/pallas_call | solution.py:246
  23.6 1.6 %collective-permute-start.7 = (bf16[4,192,128]{2,1,0:T(8,128)(2,1)S(1)}, bf16[4,192,128]{2,1,0:T(8,128)(2,1)S(1)}, u32[]{:S(2)}, u32[]{:S(2)}) collective-permute-start(bf16[4,192,128]{2,1,0:T(8,128)(2,1)S(1)} %slice.43), channel_id=1, source_target_pairs={{0,4},{2,6},{4,0},{6,2},{8,12},{10,14},{12,8},{14,10},{16,20},{18,... | collective-permute-start | bytes 589832 | tf_op jit(solution)/shard_map/ppermute | solution.py:204
  25.2 1.5 %collective-permute-start.5 = (bf16[144,2048]{1,0:T(8,128)(2,1)S(1)}, bf16[144,2048]{1,0:T(8,128)(2,1)S(1)}, u32[]{:S(2)}, u32[]{:S(2)}) collective-permute-start(bf16[144,2048]{1,0:T(8,128)(2,1)S(1)} %get-tuple-element.32), channel_id=1, source_target_pairs={{0,1},{1,0},{2,3},{3,2},{4,5},{5,4},{6,7},{7,6},{8,9},{9,8},{10,11... | collective-permute-start | bytes 1769480 | tf_op jit(solution)/shard_map/ppermute | solution.py:204
  26.7 4.2 %collective-permute-done.7 = bf16[4,192,128]{2,1,0:T(8,128)(2,1)S(1)} collective-permute-done((bf16[4,192,128]{2,1,0:T(8,128)(2,1)S(1)}, bf16[4,192,128]{2,1,0:T(8,128)(2,1)S(1)}, u32[]{:S(2)}, u32[]{:S(2)}) %collective-permute-start.7) | collective-permute-done | bytes 196640 | tf_op jit(solution)/shard_map/ppermute | solution.py:204
  31.0 0.8 %collective-permute-start.8 = (bf16[1,192,128]{2,1,0:T(8,128)(2,1)S(1)}, bf16[1,192,128]{2,1,0:T(8,128)(2,1)S(1)}, u32[]{:S(2)}, u32[]{:S(2)}) collective-permute-start(bf16[1,192,128]{2,1,0:T(8,128)(2,1)S(1)} %get-tuple-element.42), channel_id=1, source_target_pairs={{0,8},{2,10},{4,12},{6,14},{8,0},{10,2},{12,4},{14,6},{16,24},{18,... | collective-permute-start | bytes 147464 | tf_op jit(solution)/shard_map/ppermute | solution.py:204
  31.7 2.7 %collective-permute-start.10 = (bf16[1,192,128]{2,1,0:T(8,128)(2,1)S(1)}, bf16[1,192,128]{2,1,0:T(8,128)(2,1)S(1)}, u32[]{:S(2)}, u32[]{:S(2)}) collective-permute-start(bf16[1,192,128]{2,1,0:T(8,128)(2,1)S(1)} %get-tuple-element.43), channel_id=1, source_target_pairs={{0,24},{2,26},{4,28},{6,30},{8,16},{10,18},{12,20},{14,22},{16,8},... | collective-permute-start | bytes 147464 | tf_op jit(solution)/shard_map/ppermute | solution.py:204
  34.5 0.6 %collective-permute-done.8 = bf16[1,192,128]{2,1,0:T(8,128)(2,1)S(1)} collective-permute-done((bf16[1,192,128]{2,1,0:T(8,128)(2,1)S(1)}, bf16[1,192,128]{2,1,0:T(8,128)(2,1)S(1)}, u32[]{:S(2)}, u32[]{:S(2)}) %collective-permute-start.8) | collective-permute-done | bytes 49184 | tf_op jit(solution)/shard_map/ppermute | solution.py:204
  35.1 2.5 %collective-permute-done.10 = bf16[1,192,128]{2,1,0:T(8,128)(2,1)S(1)} collective-permute-done((bf16[1,192,128]{2,1,0:T(8,128)(2,1)S(1)}, bf16[1,192,128]{2,1,0:T(8,128)(2,1)S(1)}, u32[]{:S(2)}, u32[]{:S(2)}) %collective-permute-start.10) | collective-permute-done | bytes 49184 | tf_op jit(solution)/shard_map/ppermute | solution.py:204
  37.6 1.8 %collective-permute-done.9 = bf16[1,192,128]{2,1,0:T(8,128)(2,1)S(1)} collective-permute-done((bf16[1,192,128]{2,1,0:T(8,128)(2,1)S(1)}, bf16[1,192,128]{2,1,0:T(8,128)(2,1)S(1)}, u32[]{:S(2)}, u32[]{:S(2)}) %collective-permute-start.9) | collective-permute-done | bytes 49184 | tf_op jit(solution)/shard_map/ppermute | solution.py:204
  39.4 1.6 %collective-permute-start.11 = (bf16[1,192,128]{2,1,0:T(8,128)(2,1)S(1)}, bf16[1,192,128]{2,1,0:T(8,128)(2,1)S(1)}, u32[]{:S(2)}, u32[]{:S(2)}) collective-permute-start(bf16[1,192,128]{2,1,0:T(8,128)(2,1)S(1)} %get-tuple-element.38), channel_id=1, source_target_pairs={{0,1},{1,0},{2,3},{3,2},{4,5},{5,4},{6,7},{7,6},{8,9},{9,8},{10,11... | collective-permute-start | bytes 147464 | tf_op jit(solution)/shard_map/ppermute | solution.py:204
  41.0 1.0 %add_convert_fusion = bf16[144,2048]{1,0:T(8,128)(2,1)} fusion(bf16[144,2048]{1,0:T(8,128)(2,1)S(1)} %collective-permute-done.5, bf16[144,2048]{1,0:T(8,128)(2,1)S(1)} %get-tuple-element.31), kind=kLoop, calls=%fused_computation | loop fusion | flops 1179648 | bytes 1769472 | tf_op jit(solution)/shard_map/convert_element_type | solution.py:273
  42.0 1.6 %collective-permute-done.11.refs_1_ = bf16[1,192,128]{2,1,0:T(8,128)(2,1)S(1)} collective-permute-done((bf16[1,192,128]{2,1,0:T(8,128)(2,1)S(1)}, bf16[1,192,128]{2,1,0:T(8,128)(2,1)S(1)}, u32[]{:S(2)}, u32[]{:S(2)}) %collective-permute-start.11) | collective-permute-done | bytes 49184 | tf_op jit(solution)/shard_map/ppermute | solution.py:204
  43.6 0.8 %shard_map.116 = (f32[1,128,128]{2,1,0:T(8,128)}, f32[1,128,128]{2,1,0:T(8,128)}, f32[1,128,128]{2,1,0:T(8,128)}) custom-call(s32[1]{0:T(128)} %bitcast.1.rank_ref, f32[1,192,128]{2,1,0:T(8,128)S(1)} %get-tuple-element.39.refs_0_, bf16[1,192,128]{2,1,0:T(8,128)(2,1)S(1)} %collective-permute-done.11.refs_1_), custom_call_target="tpu_custom_call" | custom-call | tf_op jit(solution)/shard_map/pallas_call | solution.py:264
  (26 shorter events, 1.4 us)
Async XLA Ops:
  1.7 7.3 %collective-permute-start.2 = (bf16[1,192,128]{2,1,0:T(8,128)(2,1)S(1)}, bf16[1,192,128]{2,1,0:T(8,128)(2,1)S(1)}, u32[]{:S(2)}, u32[]{:S(2)}) collective-permute-start(bf16[1,192,128]{2,1,0:T(8,128)(2,1)S(1)} %shard_map.111), channel_id=1, source_target_pairs={{0,24},{2,26},{4,28},{6,30},{8,16},{10,18},{12,20},{14,22},{16,8},... | collective-permute-start | bytes 147464 | tf_op jit(solution)/shard_map/ppermute | solution.py:204
  6.8 5.0 %collective-permute-start.1 = (bf16[1,192,128]{2,1,0:T(8,128)(2,1)S(1)}, bf16[1,192,128]{2,1,0:T(8,128)(2,1)S(1)}, u32[]{:S(2)}, u32[]{:S(2)}) collective-permute-start(bf16[1,192,128]{2,1,0:T(8,128)(2,1)S(1)} %shard_map.111), channel_id=1, source_target_pairs={{0,16},{2,18},{4,20},{6,22},{8,24},{10,26},{12,28},{14,30},{16,0},... | collective-permute-start | bytes 147464 | tf_op jit(solution)/shard_map/ppermute | solution.py:204
  6.8 5.0 %collective-permute-start = (bf16[1,192,128]{2,1,0:T(8,128)(2,1)S(1)}, bf16[1,192,128]{2,1,0:T(8,128)(2,1)S(1)}, u32[]{:S(2)}, u32[]{:S(2)}) collective-permute-start(bf16[1,192,128]{2,1,0:T(8,128)(2,1)S(1)} %shard_map.111), channel_id=1, source_target_pairs={{0,8},{2,10},{4,12},{6,14},{8,0},{10,2},{12,4},{14,6},{16,24},{18,... | collective-permute-start | bytes 147464 | tf_op jit(solution)/shard_map/ppermute | solution.py:204
  11.8 5.8 %collective-permute-start.3 = (bf16[4,192,128]{2,1,0:T(8,128)(2,1)S(1)}, bf16[4,192,128]{2,1,0:T(8,128)(2,1)S(1)}, u32[]{:S(2)}, u32[]{:S(2)}) collective-permute-start(bf16[4,192,128]{2,1,0:T(8,128)(2,1)S(1)} %pad_maximum_fusion.w_ref), channel_id=1, source_target_pairs={{0,4},{2,6},{4,0},{6,2},{8,12},{10,14},{12,8},{14,10},{16,20},{18,... | collective-permute-start | bytes 589832 | tf_op jit(solution)/shard_map/ppermute | solution.py:204
  13.4 0.7 %copy-start.1 = (s32[16]{0:T(128)S(1)}, s32[16]{0:T(128)}, u32[]{:S(2)}) copy-start(s32[16]{0:T(128)} %in_ref.3) | copy-start | bytes 196
  14.1 0.7 %copy-start.3 = (s32[16]{0:T(128)S(1)}, s32[16]{0:T(128)}, u32[]{:S(2)}) copy-start(s32[16]{0:T(128)} %out_row_ref.1) | copy-start | bytes 196
  17.2 2.3 %copy-start = (s32[16]{0:T(128)S(1)}, s32[16]{0:T(128)}, u32[]{:S(2)}) copy-start(s32[16]{0:T(128)} %col_ref.3) | copy-start | bytes 196
  17.7 1.8 %collective-permute-start.4 = (bf16[8,192,128]{2,1,0:T(8,128)(2,1)S(1)}, bf16[8,192,128]{2,1,0:T(8,128)(2,1)S(1)}, u32[]{:S(2)}, u32[]{:S(2)}) collective-permute-start(bf16[8,192,128]{2,1,0:T(8,128)(2,1)S(1)} %constant_dynamic-update-slice_fusion.near_ref), channel_id=1, source_target_pairs={{0,2},{2,0},{4,6},{6,4},{8,10},{10,8},{12,14},{14,12},{16,18},{18,... | collective-permute-start | bytes 1179656 | tf_op jit(solution)/shard_map/ppermute | solution.py:204
  19.5 2.4 %copy-start.2 = (s32[16]{0:T(128)S(1)}, s32[16]{0:T(128)}, u32[]{:S(2)}) copy-start(s32[16]{0:T(128)} %in_ref.3) | copy-start | bytes 196
  21.6 1.8 %collective-permute-start.6 = (bf16[8,192,128]{2,1,0:T(8,128)(2,1)S(1)}, bf16[8,192,128]{2,1,0:T(8,128)(2,1)S(1)}, u32[]{:S(2)}, u32[]{:S(2)}) collective-permute-start(bf16[8,192,128]{2,1,0:T(8,128)(2,1)S(1)} %get-tuple-element.34), channel_id=1, source_target_pairs={{0,2},{2,0},{4,6},{6,4},{8,10},{10,8},{12,14},{14,12},{16,18},{18,... | collective-permute-start | bytes 1179656 | tf_op jit(solution)/shard_map/ppermute | solution.py:204
  23.6 7.3 %collective-permute-start.7 = (bf16[4,192,128]{2,1,0:T(8,128)(2,1)S(1)}, bf16[4,192,128]{2,1,0:T(8,128)(2,1)S(1)}, u32[]{:S(2)}, u32[]{:S(2)}) collective-permute-start(bf16[4,192,128]{2,1,0:T(8,128)(2,1)S(1)} %slice.43), channel_id=1, source_target_pairs={{0,4},{2,6},{4,0},{6,2},{8,12},{10,14},{12,8},{14,10},{16,20},{18,... | collective-permute-start | bytes 589832 | tf_op jit(solution)/shard_map/ppermute | solution.py:204
  25.2 15.8 %collective-permute-start.5 = (bf16[144,2048]{1,0:T(8,128)(2,1)S(1)}, bf16[144,2048]{1,0:T(8,128)(2,1)S(1)}, u32[]{:S(2)}, u32[]{:S(2)}) collective-permute-start(bf16[144,2048]{1,0:T(8,128)(2,1)S(1)} %get-tuple-element.32), channel_id=1, source_target_pairs={{0,1},{1,0},{2,3},{3,2},{4,5},{5,4},{6,7},{7,6},{8,9},{9,8},{10,11... | collective-permute-start | bytes 1769480 | tf_op jit(solution)/shard_map/ppermute | solution.py:204
  31.0 4.2 %collective-permute-start.8 = (bf16[1,192,128]{2,1,0:T(8,128)(2,1)S(1)}, bf16[1,192,128]{2,1,0:T(8,128)(2,1)S(1)}, u32[]{:S(2)}, u32[]{:S(2)}) collective-permute-start(bf16[1,192,128]{2,1,0:T(8,128)(2,1)S(1)} %get-tuple-element.42), channel_id=1, source_target_pairs={{0,8},{2,10},{4,12},{6,14},{8,0},{10,2},{12,4},{14,6},{16,24},{18,... | collective-permute-start | bytes 147464 | tf_op jit(solution)/shard_map/ppermute | solution.py:204
  31.7 5.9 %collective-permute-start.10 = (bf16[1,192,128]{2,1,0:T(8,128)(2,1)S(1)}, bf16[1,192,128]{2,1,0:T(8,128)(2,1)S(1)}, u32[]{:S(2)}, u32[]{:S(2)}) collective-permute-start(bf16[1,192,128]{2,1,0:T(8,128)(2,1)S(1)} %get-tuple-element.43), channel_id=1, source_target_pairs={{0,24},{2,26},{4,28},{6,30},{8,16},{10,18},{12,20},{14,22},{16,8},... | collective-permute-start | bytes 147464 | tf_op jit(solution)/shard_map/ppermute | solution.py:204
  34.4 5.0 %collective-permute-start.9 = (bf16[1,192,128]{2,1,0:T(8,128)(2,1)S(1)}, bf16[1,192,128]{2,1,0:T(8,128)(2,1)S(1)}, u32[]{:S(2)}, u32[]{:S(2)}) collective-permute-start(bf16[1,192,128]{2,1,0:T(8,128)(2,1)S(1)} %get-tuple-element.44), channel_id=1, source_target_pairs={{0,16},{2,18},{4,20},{6,22},{8,24},{10,26},{12,28},{14,30},{16,0},... | collective-permute-start | bytes 147464 | tf_op jit(solution)/shard_map/ppermute | solution.py:204
  39.4 4.2 %collective-permute-start.11 = (bf16[1,192,128]{2,1,0:T(8,128)(2,1)S(1)}, bf16[1,192,128]{2,1,0:T(8,128)(2,1)S(1)}, u32[]{:S(2)}, u32[]{:S(2)}) collective-permute-start(bf16[1,192,128]{2,1,0:T(8,128)(2,1)S(1)} %get-tuple-element.38), channel_id=1, source_target_pairs={{0,1},{1,0},{2,3},{3,2},{4,5},{5,4},{6,7},{7,6},{8,9},{9,8},{10,11... | collective-permute-start | bytes 147464 | tf_op jit(solution)/shard_map/ppermute | solution.py:204

commit v4 on v3

--- a/solution.py
+++ b/solution.py
@@ -6,6 +6,7 @@
 from jax.experimental import pallas as pl
 from jax.experimental.pallas import tpu as pltpu
 from jax.sharding import PartitionSpec as P
+
 
 VMEM = pltpu.MemorySpace.VMEM
 SMEM = pltpu.MemorySpace.SMEM
@@ -68,34 +69,21 @@
     grad_ref[at, two:] = dot(hidden, cot, 1, 0).astype(BF16)
 
 
-def first_kernel(me_ref, in_ref, out_row_ref, tokens, cotangent, w_ref, tok_ref, cot_ref, gu_ref, dh_ref, sems, *, local):
-    count, _, block = tok_ref.shape
-    slots = Slots(me_ref[0], count, local)
-
-    def column(array, index):
-        return array.at[:, pl.ds(pl.multiple_of(index * block, block), block)]
-
+def collect_kernel(me_ref, index_ref, array, out_ref, sems, *, local):
+    count, _, block = out_ref.shape
     copies = []
-    for slot, key in enumerate(slots.keys):
-        copies.append(
-            (
-                pltpu.make_async_copy(column(tokens, in_ref[key]), tok_ref.at[slot], sems.at[0, slot]),
-                pltpu.make_async_copy(column(cotangent, out_row_ref[key]), cot_ref.at[slot], sems.at[1, slot]),
-            )
-        )
-        for copy in copies[-1]:
-            copy.start()
-    for pair in copies:
-        for copy in pair:
-            copy.wait()
-    for slot in range(slots.quarter):
-        forward(w_ref, slot, tok_ref[slot], cot_ref[slot], gu_ref, dh_ref, slot)
-
-
-def second_kernel(w_ref, tok_ref, cot_ref, gu_ref, dh_ref):
-    quarter = w_ref.shape[0]
-    for slot in range(quarter):
-        forward(w_ref, slot, tok_ref[quarter + slot], cot_ref[quarter + slot], gu_ref, dh_ref, slot)
+    for slot, key in enumerate(Slots(me_ref[0], count, local).keys):
+        at = pl.ds(pl.multiple_of(index_ref[key] * block, block), block)
+        copies.append(pltpu.make_async_copy(array.at[:, at], out_ref.at[slot], sems.at[slot]))
+    for copy in copies:
+        copy.start()
+    for copy in copies:
+        copy.wait()
+
+
+def forward_kernel(w_ref, tok_ref, cot_ref, gu_ref, dh_ref, *, first):
+    for slot in range(w_ref.shape[0]):
+        forward(w_ref, slot, tok_ref[first + slot], cot_ref[first + slot], gu_ref, dh_ref, slot)
 
 
 def third_kernel(
@@ -219,21 +207,35 @@
             pltpu.SemaphoreType.DMA((3,)),
         ],
     )(rank, *map(outside, (gate_blocks, up_blocks, down_blocks)))
-    column = jnp.concatenate([own] + [over(own, 4 * i) for i in range(1, fars)], axis=0)
-    beside = over(column, 2)
-    some_gu, some_dh = f32(quarter, two, token_count), f32(quarter, share, token_count)
-    tok, cot, gu0, dh0 = call(
-        functools.partial(first_kernel, local=local),
-        [bf16(count, token_count, block)] * 2 + [some_gu, some_dh],
-        "ssshhv",
-        [pltpu.SemaphoreType.DMA((2, count))],
-        8,
-        macs * quarter,
-    )(me, in_row, out_row, outside(tokens), outside(cotangent), column)
-    beside, tok = lax.optimization_barrier((beside, tok))
+    across_z = [over(own, 4 * i) for i in range(1, fars)]
+    beside_own, beside_next = over(own, 2), over(own, 6)
+    column = jnp.concatenate([own] + across_z, axis=0)
+    onward = over(jnp.concatenate(across_z[1:], axis=0), 2)
+    beside = jnp.concatenate([beside_own, beside_next, onward], axis=0)
+
+    def collect(array, index):
+        return call(
+            functools.partial(collect_kernel, local=local),
+            bf16(count, token_count, block),
+            "ssh",
+            [pltpu.SemaphoreType.DMA((count,))],
+            4,
+            macs * quarter,
+        )(me, outside(index), outside(array))
+
+    tok = collect(tokens, in_row)
+    cot = collect(cotangent, out_row)
+
+    def some_forward(weights, index):
+        kernel = functools.partial(forward_kernel, first=index * quarter)
+        out = [f32(quarter, two, token_count), f32(quarter, share, token_count)]
+        return call(kernel, out, "vvv", (), 8, macs * quarter)(weights, tok, cot)
+
+    gu0, dh0 = some_forward(column, 0)
+    beside, gu0 = lax.optimization_barrier((beside, gu0))
     near = jnp.concatenate([column, beside], axis=0)
     far = over(near, 1)
-    gu1, dh1 = call(second_kernel, [some_gu, some_dh], "vvv", (), 8, macs * quarter)(beside, tok, cot)
+    gu1, dh1 = some_forward(beside, 1)
     grad_parts = bf16(2 * quarter, rows, block)
     far_grad, gu_grad, hidden = call(
         functools.partial(third_kernel, local=local),
@@ -254,23 +256,26 @@
 
     arrived = [across(spread[d], d) for d in range(1, ranks)]
     chip = near_grad.astype(F32) + over(far_grad, 1).astype(F32)
-    plane = chip[:quarter] + over(chip[quarter:].astype(BF16), 2).astype(F32)
-    summed = plane[:local]
-    for i in range(1, fars):
-        piece = plane[i * local : (i + 1) * local].astype(BF16)
-        summed = summed + over(piece, 4 * i).astype(F32)
+    onward = over(chip[quarter + 2 * local :].astype(BF16), 2).astype(F32)
+    summed = chip[:local]
+    for i in range(2, fars):
+        piece = chip[i * local : (i + 1) * local] + onward[(i - 2) * local : (i - 1) * local]
+        summed = summed + over(piece.astype(BF16), 4 * i).astype(F32)
+    for first, d in ((local, 4), (quarter, 2), (quarter + local, 6)):
+        summed = summed + over(chip[first : first + local].astype(BF16), d).astype(F32)
     summed = summed * scale
     pieces = [summed] + [across(summed.astype(BF16), d) for d in range(1, ranks)]
+    input_grad = spread[0].astype(F32)
+    for piece in arrived:
+        input_grad = input_grad + piece.astype(F32)
+    input_grad, *pieces = lax.optimization_barrier((input_grad.astype(BF16), *pieces))
     gate_grads, up_grads, down_grads = call(
         functools.partial(place_kernel, ranks=ranks),
         [f32(local, block, block)] * 3,
         "s" + "v" * ranks,
         [pltpu.VMEM((block, block), F32)],
     )(rank, *pieces)
-    input_grad = spread[0].astype(F32)
-    for piece in arrived:
-        input_grad = input_grad + piece.astype(F32)
-    return input_grad.astype(BF16), gate_grads, up_grads, down_grads
+    return input_grad, gate_grads, up_grads, down_grads
 
 
 def solution(mesh):

time: 44.7 us -> 45 us (level)
  waiting for transfers between devices: 16.8 us -> 11.3 us
  starting transfers between devices: 15.8 us -> 21.1 us
  Pallas kernels: 8.4 us -> 10.1 us
  local copies, waits for them, and re-layouts: 1.43 us -> 0.09 us
    ppermute x12 -> x16, waiting for transfers between devices: 16.8 us -> 11.3 us  [along(): return lax.ppermute(x, axis, [(i, i ^ d) for i in range(size)])]
    ppermute x12 -> x16, starting transfers between devices: 15.8 us -> 21.1 us  [along(): return lax.ppermute(x, axis, [(i, i ^ d) for i in range(size)])]
    pallas_call x2 -> x4, Pallas kernels: 2.8 us -> 4.46 us  [the longest x2 3.8 us: collect(): call(functools.partial(collect_kernel, local=local), bf16(count, token_co...]
    unnamed x12 -> x8, local copies, waits for them, and re-layouts: 1.36 us -> 0.05 us
    convert_element_type x1 -> x3, other arithmetic: 0.97 us -> 1 us  [the longest x1 0.97 us: on_device(): input_grad.astype(BF16)]
  transfers between devices with their start and end apart: 12 -> 16, of which waited for: 9 -> 6; matrix products, arithmetic and copies ran while one was open for 2% -> 3% of each run, Pallas kernels for 10% -> 14%
where the time goes in v4:
time: 45 us; the launch traced here: 44.6 us
  starting transfers between devices  21.1 us (47%)
  waiting for transfers between devices  11.3 us (25%)
  Pallas kernels  10.1 us (22%)
  other arithmetic  1.23 us (3%)
  between operations  0.81 us (2%)
    ppermute x16, starting transfers between devices, along(): return lax.ppermute(x, axis, [(i, i ^ d) for i in range(size)])  21.1 us
    ppermute x16, waiting for transfers between devices, along(): return lax.ppermute(x, axis, [(i, i ^ d) for i in range(size)])  11.3 us
    pallas_call x2, Pallas kernels, collect(): call(functools.partial(collect_kernel, local=local), bf16(count, token_co...  3.8 us
    pallas_call x1, Pallas kernels, on_device(): call(functools.partial(third_kernel, local=local), [grad_parts, bf16(coun...  2.17 us
    pallas_call x1, Pallas kernels, on_device(): call(functools.partial(fourth_kernel, ranks=ranks, local=local), [bf16(to...  1.65 us
    pallas_call x1, Pallas kernels, on_device(): call(pack_kernel, bf16(local, rows, block), 'shhh', [pltpu.VMEM((3, local...  1.01 us
    convert_element_type x1, other arithmetic, on_device(): input_grad.astype(BF16)  0.97 us
  transfers between devices with their start and end apart: 16, of which 6 were waited for; matrix products, arithmetic and copies ran while one was open for 3% of the time, Pallas kernels for 14%

profile of v4, /device:TPU:0, one launch (start us, length us, event | category | flops | bytes accessed | tf_op | source)
XLA Modules:
  0.0 44.6 jit_solution(6921570847028593268)
XLA Ops:
  0.6 1.0 %shard_map.111 = bf16[1,192,128]{2,1,0:T(8,128)(2,1)S(1)} custom-call(s32[1]{0:T(128)} %bitcast.1.rank_ref, bf16[1,128,128]{2,1,0:T(8,128)(2,1)} %gate_ref.1, bf16[1,128,128]{2,1,0:T(8,128)(2,1)} %up_ref.1, bf16[1,128,128]{2,1,0:T(8,128)(2,1)} %down_ref.1), custom_call_target="tpu_custom_call" | custom-call | tf_op jit(solution)/shard_map/pallas_call | solution.py:200
  1.7 4.1 %collective-permute-start.4 = (bf16[1,192,128]{2,1,0:T(8,128)(2,1)S(1)}, bf16[1,192,128]{2,1,0:T(8,128)(2,1)S(1)}, u32[]{:S(2)}, u32[]{:S(2)}) collective-permute-start(bf16[1,192,128]{2,1,0:T(8,128)(2,1)S(1)} %shard_map.111), channel_id=1, source_target_pairs={{0,12},{2,14},{4,8},{6,10},{8,4},{10,6},{12,0},{14,2},{16,28},{18,... | collective-permute-start | bytes 147464 | tf_op jit(solution)/shard_map/ppermute | solution.py:192
  6.2 2.5 %collective-permute-start.2 = (bf16[1,192,128]{2,1,0:T(8,128)(2,1)S(1)}, bf16[1,192,128]{2,1,0:T(8,128)(2,1)S(1)}, u32[]{:S(2)}, u32[]{:S(2)}) collective-permute-start(bf16[1,192,128]{2,1,0:T(8,128)(2,1)S(1)} %shard_map.111), channel_id=1, source_target_pairs={{0,24},{2,26},{4,28},{6,30},{8,16},{10,18},{12,20},{14,22},{16,8},... | collective-permute-start | bytes 147464 | tf_op jit(solution)/shard_map/ppermute | solution.py:192
  8.8 1.8 %collective-permute-start = (bf16[1,192,128]{2,1,0:T(8,128)(2,1)S(1)}, bf16[1,192,128]{2,1,0:T(8,128)(2,1)S(1)}, u32[]{:S(2)}, u32[]{:S(2)}) collective-permute-start(bf16[1,192,128]{2,1,0:T(8,128)(2,1)S(1)} %shard_map.111), channel_id=1, source_target_pairs={{0,8},{2,10},{4,12},{6,14},{8,0},{10,2},{12,4},{14,6},{16,24},{18,... | collective-permute-start | bytes 147464 | tf_op jit(solution)/shard_map/ppermute | solution.py:192
  10.6 1.9 %shard_map.112.tok_ref = bf16[16,144,128]{2,1,0:T(8,128)(2,1)S(1)} custom-call(s32[1]{0:T(128)} %bitcast.me_ref, s32[16]{0:T(128)} %in_ref.1, bf16[144,4096]{1,0:T(8,128)(2,1)} %array.2), custom_call_target="tpu_custom_call" | custom-call | flops 28311552 | bytes 110592 | tf_op jit(solution)/shard_map/pallas_call | solution.py:217
  12.6 1.9 %shard_map.113.cot_ref = bf16[16,144,128]{2,1,0:T(8,128)(2,1)S(1)} custom-call(s32[1]{0:T(128)} %bitcast.me_ref, s32[16]{0:T(128)} %index_ref.3, bf16[144,4096]{1,0:T(8,128)(2,1)} %array.3), custom_call_target="tpu_custom_call" | custom-call | flops 28311552 | bytes 110592 | tf_op jit(solution)/shard_map/pallas_call | solution.py:217
  14.5 1.6 %collective-permute-start.5 = (bf16[2,192,128]{2,1,0:T(8,128)(2,1)S(1)}, bf16[2,192,128]{2,1,0:T(8,128)(2,1)S(1)}, u32[]{:S(2)}, u32[]{:S(2)}) collective-permute-start(bf16[2,192,128]{2,1,0:T(8,128)(2,1)S(1)} %pad_maximum_fusion.2), channel_id=1, source_target_pairs={{0,4},{2,6},{4,0},{6,2},{8,12},{10,14},{12,8},{14,10},{16,20},{18,... | collective-permute-start | bytes 294920 | tf_op jit(solution)/shard_map/ppermute | solution.py:192
  16.5 2.6 %collective-permute-done.5 = bf16[2,192,128]{2,1,0:T(8,128)(2,1)S(1)} collective-permute-done((bf16[2,192,128]{2,1,0:T(8,128)(2,1)S(1)}, bf16[2,192,128]{2,1,0:T(8,128)(2,1)S(1)}, u32[]{:S(2)}, u32[]{:S(2)}) %collective-permute-start.5) | collective-permute-done | bytes 98336 | tf_op jit(solution)/shard_map/ppermute | solution.py:192
  19.6 1.4 %collective-permute-done.6.w_ref.far_ref = bf16[8,192,128]{2,1,0:T(8,128)(2,1)S(1)} collective-permute-done((bf16[8,192,128]{2,1,0:T(8,128)(2,1)S(1)}, bf16[8,192,128]{2,1,0:T(8,128)(2,1)S(1)}, u32[]{:S(2)}, u32[]{:S(2)}) %collective-permute-start.6) | collective-permute-done | bytes 393248 | tf_op jit(solution)/shard_map/ppermute | solution.py:192
  21.0 2.2 %shard_map.116 = (bf16[8,192,128]{2,1,0:T(8,128)(2,1)S(1)}, bf16[16,128,144]{2,1,0:T(8,128)(2,1)S(1)}, bf16[16,64,144]{2,1,0:T(8,128)(2,1)S(1)}) custom-call(s32[1]{0:T(128)} %bitcast.me_ref, s32[16]{0:T(128)S(1)} %copy-done, bf16[8,192,128]{2,1,0:T(8,128)(2,1)S(1)} %collective-permute-done.6.w_ref.far_ref, bf16[16,144,128]{2,1,0:T(8,128)(2,1)S(1)} %shard_map.112.tok_ref, ...), custom_call_target="tpu_custom_call" | custom-call | flops 113246208 | bytes 442368 | tf_op jit(solution)/shard_map/pallas_call | solution.py:240
  23.4 1.6 %shard_map.117 = (bf16[144,2048]{1,0:T(8,128)(2,1)S(1)}, bf16[144,2048]{1,0:T(8,128)(2,1)S(1)}, bf16[8,192,128]{2,1,0:T(8,128)(2,1)S(1)}) custom-call(s32[1]{0:T(128)} %bitcast.me_ref, s32[1]{0:T(128)} %bitcast.1.rank_ref, s32[16]{0:T(128)S(1)} %copy-done, s32[16]{0:T(128)S(1)} %copy-done.1, ...), custom_call_target="tpu_custom_call" | custom-call | flops 113246208 | bytes 442368 | tf_op jit(solution)/shard_map/pallas_call | solution.py:248
  25.1 1.6 %collective-permute-start.7 = (bf16[144,2048]{1,0:T(8,128)(2,1)S(1)}, bf16[144,2048]{1,0:T(8,128)(2,1)S(1)}, u32[]{:S(2)}, u32[]{:S(2)}) collective-permute-start(bf16[144,2048]{1,0:T(8,128)(2,1)S(1)} %get-tuple-element.31), channel_id=1, source_target_pairs={{0,1},{1,0},{2,3},{3,2},{4,5},{5,4},{6,7},{7,6},{8,9},{9,8},{10,11... | collective-permute-start | bytes 1769480 | tf_op jit(solution)/shard_map/ppermute | solution.py:192
  26.8 1.6 %collective-permute-start.9 = (bf16[2,192,128]{2,1,0:T(8,128)(2,1)S(1)}, bf16[2,192,128]{2,1,0:T(8,128)(2,1)S(1)}, u32[]{:S(2)}, u32[]{:S(2)}) collective-permute-start(bf16[2,192,128]{2,1,0:T(8,128)(2,1)S(1)} %slice.42), channel_id=1, source_target_pairs={{0,4},{2,6},{4,0},{6,2},{8,12},{10,14},{12,8},{14,10},{16,20},{18,... | collective-permute-start | bytes 294920 | tf_op jit(solution)/shard_map/ppermute | solution.py:192
  28.6 1.7 %collective-permute-start.14 = (bf16[1,192,128]{2,1,0:T(8,128)(2,1)S(1)}, bf16[1,192,128]{2,1,0:T(8,128)(2,1)S(1)}, u32[]{:S(2)}, u32[]{:S(2)}) collective-permute-start(bf16[1,192,128]{2,1,0:T(8,128)(2,1)S(1)} %get-tuple-element.47), channel_id=1, source_target_pairs={{0,12},{2,14},{4,8},{6,10},{8,4},{10,6},{12,0},{14,2},{16,28},{18,... | collective-permute-start | bytes 147464 | tf_op jit(solution)/shard_map/ppermute | solution.py:192
  30.4 1.5 %collective-permute-start.13 = (bf16[1,192,128]{2,1,0:T(8,128)(2,1)S(1)}, bf16[1,192,128]{2,1,0:T(8,128)(2,1)S(1)}, u32[]{:S(2)}, u32[]{:S(2)}) collective-permute-start(bf16[1,192,128]{2,1,0:T(8,128)(2,1)S(1)} %get-tuple-element.48), channel_id=1, source_target_pairs={{0,4},{2,6},{4,0},{6,2},{8,12},{10,14},{12,8},{14,10},{16,20},{18,... | collective-permute-start | bytes 147464 | tf_op jit(solution)/shard_map/ppermute | solution.py:192
  32.0 1.8 %collective-permute-start.10 = (bf16[1,192,128]{2,1,0:T(8,128)(2,1)S(1)}, bf16[1,192,128]{2,1,0:T(8,128)(2,1)S(1)}, u32[]{:S(2)}, u32[]{:S(2)}) collective-permute-start(bf16[1,192,128]{2,1,0:T(8,128)(2,1)S(1)} %get-tuple-element.42), channel_id=1, source_target_pairs={{0,16},{2,18},{4,20},{6,22},{8,24},{10,26},{12,28},{14,30},{16,0},... | collective-permute-start | bytes 147464 | tf_op jit(solution)/shard_map/ppermute | solution.py:192
  33.7 1.3 %collective-permute-start.11 = (bf16[1,192,128]{2,1,0:T(8,128)(2,1)S(1)}, bf16[1,192,128]{2,1,0:T(8,128)(2,1)S(1)}, u32[]{:S(2)}, u32[]{:S(2)}) collective-permute-start(bf16[1,192,128]{2,1,0:T(8,128)(2,1)S(1)} %get-tuple-element.43), channel_id=1, source_target_pairs={{0,24},{2,26},{4,28},{6,30},{8,16},{10,18},{12,20},{14,22},{16,8},... | collective-permute-start | bytes 147464 | tf_op jit(solution)/shard_map/ppermute | solution.py:192
  35.0 2.9 %collective-permute-done.10 = bf16[1,192,128]{2,1,0:T(8,128)(2,1)S(1)} collective-permute-done((bf16[1,192,128]{2,1,0:T(8,128)(2,1)S(1)}, bf16[1,192,128]{2,1,0:T(8,128)(2,1)S(1)}, u32[]{:S(2)}, u32[]{:S(2)}) %collective-permute-start.10) | collective-permute-done | bytes 49184 | tf_op jit(solution)/shard_map/ppermute | solution.py:192
  37.9 1.7 %collective-permute-done.11 = bf16[1,192,128]{2,1,0:T(8,128)(2,1)S(1)} collective-permute-done((bf16[1,192,128]{2,1,0:T(8,128)(2,1)S(1)}, bf16[1,192,128]{2,1,0:T(8,128)(2,1)S(1)}, u32[]{:S(2)}, u32[]{:S(2)}) %collective-permute-start.11) | collective-permute-done | bytes 49184 | tf_op jit(solution)/shard_map/ppermute | solution.py:192
  39.7 0.6 %collective-permute-start.15 = (bf16[1,192,128]{2,1,0:T(8,128)(2,1)S(1)}, bf16[1,192,128]{2,1,0:T(8,128)(2,1)S(1)}, u32[]{:S(2)}, u32[]{:S(2)}) collective-permute-start(bf16[1,192,128]{2,1,0:T(8,128)(2,1)S(1)} %get-tuple-element.40), channel_id=1, source_target_pairs={{0,1},{1,0},{2,3},{3,2},{4,5},{5,4},{6,7},{7,6},{8,9},{9,8},{10,11... | collective-permute-start | bytes 147464 | tf_op jit(solution)/shard_map/ppermute | solution.py:192
  40.3 1.0 %collective-permute-done.7 = bf16[144,2048]{1,0:T(8,128)(2,1)S(1)} collective-permute-done((bf16[144,2048]{1,0:T(8,128)(2,1)S(1)}, bf16[144,2048]{1,0:T(8,128)(2,1)S(1)}, u32[]{:S(2)}, u32[]{:S(2)}) %collective-permute-start.7) | collective-permute-done | bytes 589856 | tf_op jit(solution)/shard_map/ppermute | solution.py:192
  41.2 1.0 %add_convert_fusion = bf16[144,2048]{1,0:T(8,128)(2,1)} fusion(bf16[144,2048]{1,0:T(8,128)(2,1)S(1)} %collective-permute-done.7, bf16[144,2048]{1,0:T(8,128)(2,1)S(1)} %get-tuple-element.30), kind=kLoop, calls=%fused_computation | loop fusion | flops 1179648 | bytes 1769472 | tf_op jit(solution)/shard_map/convert_element_type | solution.py:271
  42.2 1.6 %collective-permute-done.15.refs_1_ = bf16[1,192,128]{2,1,0:T(8,128)(2,1)S(1)} collective-permute-done((bf16[1,192,128]{2,1,0:T(8,128)(2,1)S(1)}, bf16[1,192,128]{2,1,0:T(8,128)(2,1)S(1)}, u32[]{:S(2)}, u32[]{:S(2)}) %collective-permute-start.15) | collective-permute-done | bytes 49184 | tf_op jit(solution)/shard_map/ppermute | solution.py:192
  43.8 0.8 %shard_map.118 = (f32[1,128,128]{2,1,0:T(8,128)}, f32[1,128,128]{2,1,0:T(8,128)}, f32[1,128,128]{2,1,0:T(8,128)}) custom-call(s32[1]{0:T(128)} %bitcast.1.rank_ref, f32[1,192,128]{2,1,0:T(8,128)S(1)} %get-tuple-element.35.refs_0_, bf16[1,192,128]{2,1,0:T(8,128)(2,1)S(1)} %collective-permute-done.15.refs_1_), custom_call_target="tpu_custom_call" | custom-call | tf_op jit(solution)/shard_map/pallas_call | solution.py:272
  (35 shorter events, 2.2 us)
Async XLA Ops:
  1.7 14.8 %collective-permute-start.4 = (bf16[1,192,128]{2,1,0:T(8,128)(2,1)S(1)}, bf16[1,192,128]{2,1,0:T(8,128)(2,1)S(1)}, u32[]{:S(2)}, u32[]{:S(2)}) collective-permute-start(bf16[1,192,128]{2,1,0:T(8,128)(2,1)S(1)} %shard_map.111), channel_id=1, source_target_pairs={{0,12},{2,14},{4,8},{6,10},{8,4},{10,6},{12,0},{14,2},{16,28},{18,... | collective-permute-start | bytes 147464 | tf_op jit(solution)/shard_map/ppermute | solution.py:192
  5.7 10.8 %collective-permute-start.3 = (bf16[1,192,128]{2,1,0:T(8,128)(2,1)S(1)}, bf16[1,192,128]{2,1,0:T(8,128)(2,1)S(1)}, u32[]{:S(2)}, u32[]{:S(2)}) collective-permute-start(bf16[1,192,128]{2,1,0:T(8,128)(2,1)S(1)} %shard_map.111), channel_id=1, source_target_pairs={{0,4},{2,6},{4,0},{6,2},{8,12},{10,14},{12,8},{14,10},{16,20},{18,... | collective-permute-start | bytes 147464 | tf_op jit(solution)/shard_map/ppermute | solution.py:192
  6.2 8.2 %collective-permute-start.2 = (bf16[1,192,128]{2,1,0:T(8,128)(2,1)S(1)}, bf16[1,192,128]{2,1,0:T(8,128)(2,1)S(1)}, u32[]{:S(2)}, u32[]{:S(2)}) collective-permute-start(bf16[1,192,128]{2,1,0:T(8,128)(2,1)S(1)} %shard_map.111), channel_id=1, source_target_pairs={{0,24},{2,26},{4,28},{6,30},{8,16},{10,18},{12,20},{14,22},{16,8},... | collective-permute-start | bytes 147464 | tf_op jit(solution)/shard_map/ppermute | solution.py:192
  8.7 5.7 %collective-permute-start.1 = (bf16[1,192,128]{2,1,0:T(8,128)(2,1)S(1)}, bf16[1,192,128]{2,1,0:T(8,128)(2,1)S(1)}, u32[]{:S(2)}, u32[]{:S(2)}) collective-permute-start(bf16[1,192,128]{2,1,0:T(8,128)(2,1)S(1)} %shard_map.111), channel_id=1, source_target_pairs={{0,16},{2,18},{4,20},{6,22},{8,24},{10,26},{12,28},{14,30},{16,0},... | collective-permute-start | bytes 147464 | tf_op jit(solution)/shard_map/ppermute | solution.py:192
  8.8 7.2 %collective-permute-start = (bf16[1,192,128]{2,1,0:T(8,128)(2,1)S(1)}, bf16[1,192,128]{2,1,0:T(8,128)(2,1)S(1)}, u32[]{:S(2)}, u32[]{:S(2)}) collective-permute-start(bf16[1,192,128]{2,1,0:T(8,128)(2,1)S(1)} %shard_map.111), channel_id=1, source_target_pairs={{0,8},{2,10},{4,12},{6,14},{8,0},{10,2},{12,4},{14,6},{16,24},{18,... | collective-permute-start | bytes 147464 | tf_op jit(solution)/shard_map/ppermute | solution.py:192
  14.5 4.7 %collective-permute-start.5 = (bf16[2,192,128]{2,1,0:T(8,128)(2,1)S(1)}, bf16[2,192,128]{2,1,0:T(8,128)(2,1)S(1)}, u32[]{:S(2)}, u32[]{:S(2)}) collective-permute-start(bf16[2,192,128]{2,1,0:T(8,128)(2,1)S(1)} %pad_maximum_fusion.2), channel_id=1, source_target_pairs={{0,4},{2,6},{4,0},{6,2},{8,12},{10,14},{12,8},{14,10},{16,20},{18,... | collective-permute-start | bytes 294920 | tf_op jit(solution)/shard_map/ppermute | solution.py:192
  16.5 4.5 %copy-start = (s32[16]{0:T(128)S(1)}, s32[16]{0:T(128)}, u32[]{:S(2)}) copy-start(s32[16]{0:T(128)} %col_ref.3) | copy-start | bytes 196
  19.2 1.8 %collective-permute-start.6 = (bf16[8,192,128]{2,1,0:T(8,128)(2,1)S(1)}, bf16[8,192,128]{2,1,0:T(8,128)(2,1)S(1)}, u32[]{:S(2)}, u32[]{:S(2)}) collective-permute-start(bf16[8,192,128]{2,1,0:T(8,128)(2,1)S(1)} %constant_dynamic-update-slice_fusion.near_ref), channel_id=1, source_target_pairs={{0,2},{2,0},{4,6},{6,4},{8,10},{10,8},{12,14},{14,12},{16,18},{18,... | collective-permute-start | bytes 1179656 | tf_op jit(solution)/shard_map/ppermute | solution.py:192
  21.0 2.4 %copy-start.1 = (s32[16]{0:T(128)S(1)}, s32[16]{0:T(128)}, u32[]{:S(2)}) copy-start(s32[16]{0:T(128)} %in_ref.1) | copy-start | bytes 196
  23.2 3.4 %collective-permute-start.8 = (bf16[8,192,128]{2,1,0:T(8,128)(2,1)S(1)}, bf16[8,192,128]{2,1,0:T(8,128)(2,1)S(1)}, u32[]{:S(2)}, u32[]{:S(2)}) collective-permute-start(bf16[8,192,128]{2,1,0:T(8,128)(2,1)S(1)} %get-tuple-element.33), channel_id=1, source_target_pairs={{0,2},{2,0},{4,6},{6,4},{8,10},{10,8},{12,14},{14,12},{16,18},{18,... | collective-permute-start | bytes 1179656 | tf_op jit(solution)/shard_map/ppermute | solution.py:192
  25.1 16.2 %collective-permute-start.7 = (bf16[144,2048]{1,0:T(8,128)(2,1)S(1)}, bf16[144,2048]{1,0:T(8,128)(2,1)S(1)}, u32[]{:S(2)}, u32[]{:S(2)}) collective-permute-start(bf16[144,2048]{1,0:T(8,128)(2,1)S(1)} %get-tuple-element.31), channel_id=1, source_target_pairs={{0,1},{1,0},{2,3},{3,2},{4,5},{5,4},{6,7},{7,6},{8,9},{9,8},{10,11... | collective-permute-start | bytes 1769480 | tf_op jit(solution)/shard_map/ppermute | solution.py:192
  26.8 5.2 %collective-permute-start.9 = (bf16[2,192,128]{2,1,0:T(8,128)(2,1)S(1)}, bf16[2,192,128]{2,1,0:T(8,128)(2,1)S(1)}, u32[]{:S(2)}, u32[]{:S(2)}) collective-permute-start(bf16[2,192,128]{2,1,0:T(8,128)(2,1)S(1)} %slice.42), channel_id=1, source_target_pairs={{0,4},{2,6},{4,0},{6,2},{8,12},{10,14},{12,8},{14,10},{16,20},{18,... | collective-permute-start | bytes 294920 | tf_op jit(solution)/shard_map/ppermute | solution.py:192
  28.4 5.4 %collective-permute-start.12 = (bf16[1,192,128]{2,1,0:T(8,128)(2,1)S(1)}, bf16[1,192,128]{2,1,0:T(8,128)(2,1)S(1)}, u32[]{:S(2)}, u32[]{:S(2)}) collective-permute-start(bf16[1,192,128]{2,1,0:T(8,128)(2,1)S(1)} %get-tuple-element.46), channel_id=1, source_target_pairs={{0,8},{2,10},{4,12},{6,14},{8,0},{10,2},{12,4},{14,6},{16,24},{18,... | collective-permute-start | bytes 147464 | tf_op jit(solution)/shard_map/ppermute | solution.py:192
  28.6 6.3 %collective-permute-start.14 = (bf16[1,192,128]{2,1,0:T(8,128)(2,1)S(1)}, bf16[1,192,128]{2,1,0:T(8,128)(2,1)S(1)}, u32[]{:S(2)}, u32[]{:S(2)}) collective-permute-start(bf16[1,192,128]{2,1,0:T(8,128)(2,1)S(1)} %get-tuple-element.47), channel_id=1, source_target_pairs={{0,12},{2,14},{4,8},{6,10},{8,4},{10,6},{12,0},{14,2},{16,28},{18,... | collective-permute-start | bytes 147464 | tf_op jit(solution)/shard_map/ppermute | solution.py:192
  30.4 4.6 %collective-permute-start.13 = (bf16[1,192,128]{2,1,0:T(8,128)(2,1)S(1)}, bf16[1,192,128]{2,1,0:T(8,128)(2,1)S(1)}, u32[]{:S(2)}, u32[]{:S(2)}) collective-permute-start(bf16[1,192,128]{2,1,0:T(8,128)(2,1)S(1)} %get-tuple-element.48), channel_id=1, source_target_pairs={{0,4},{2,6},{4,0},{6,2},{8,12},{10,14},{12,8},{14,10},{16,20},{18,... | collective-permute-start | bytes 147464 | tf_op jit(solution)/shard_map/ppermute | solution.py:192
  32.0 5.9 %collective-permute-start.10 = (bf16[1,192,128]{2,1,0:T(8,128)(2,1)S(1)}, bf16[1,192,128]{2,1,0:T(8,128)(2,1)S(1)}, u32[]{:S(2)}, u32[]{:S(2)}) collective-permute-start(bf16[1,192,128]{2,1,0:T(8,128)(2,1)S(1)} %get-tuple-element.42), channel_id=1, source_target_pairs={{0,16},{2,18},{4,20},{6,22},{8,24},{10,26},{12,28},{14,30},{16,0},... | collective-permute-start | bytes 147464 | tf_op jit(solution)/shard_map/ppermute | solution.py:192
  33.7 5.9 %collective-permute-start.11 = (bf16[1,192,128]{2,1,0:T(8,128)(2,1)S(1)}, bf16[1,192,128]{2,1,0:T(8,128)(2,1)S(1)}, u32[]{:S(2)}, u32[]{:S(2)}) collective-permute-start(bf16[1,192,128]{2,1,0:T(8,128)(2,1)S(1)} %get-tuple-element.43), channel_id=1, source_target_pairs={{0,24},{2,26},{4,28},{6,30},{8,16},{10,18},{12,20},{14,22},{16,8},... | collective-permute-start | bytes 147464 | tf_op jit(solution)/shard_map/ppermute | solution.py:192
  39.7 4.2 %collective-permute-start.15 = (bf16[1,192,128]{2,1,0:T(8,128)(2,1)S(1)}, bf16[1,192,128]{2,1,0:T(8,128)(2,1)S(1)}, u32[]{:S(2)}, u32[]{:S(2)}) collective-permute-start(bf16[1,192,128]{2,1,0:T(8,128)(2,1)S(1)} %get-tuple-element.40), channel_id=1, source_target_pairs={{0,1},{1,0},{2,3},{3,2},{4,5},{5,4},{6,7},{7,6},{8,9},{9,8},{10,11... | collective-permute-start | bytes 147464 | tf_op jit(solution)/shard_map/ppermute | solution.py:192

commit v5 on v4

v5 whole, which is shorter than its diff:
```python
import functools

import jax
import jax.numpy as jnp
from jax import lax
from jax.experimental import pallas as pl
from jax.experimental.pallas import tpu as pltpu
from jax.sharding import PartitionSpec as P


VMEM = pltpu.MemorySpace.VMEM
SMEM = pltpu.MemorySpace.SMEM
HBM = pltpu.MemorySpace.HBM
F32 = jnp.float32
BF16 = jnp.bfloat16


def dot(a, b, dim_a, dim_b):
    return lax.dot_general(a, b, (((dim_a,), (dim_b,)), ((), ())), preferred_element_type=F32)


def pack_kernel(gate_ref, up_ref, down_ref, out_ref, held, turned, sems):
    share = out_ref.shape[1] // 3
    first = pl.multiple_of(lax.axis_index("mp") * share, share)
    copies = [
        pltpu.make_async_copy(ref, held.at[part], sems.at[part])
        for part, ref in enumerate((gate_ref, up_ref, down_ref))
    ]
    for copy in copies:
        copy.start()
    for part, copy in enumerate(copies):
        copy.wait()
        for i in range(out_ref.shape[0]):
            whole = held[part, i].astype(F32)
            turned[...] = whole if part == 2 else whole.T
            out_ref[i, part * share : (part + 1) * share] = turned[pl.ds(first, share), :].astype(BF16)


class Slots:
    def __init__(self, count, local):
        me = lax.axis_index("dp")
        self.count, self.half, self.quarter = count, count // 2, count // 4
        self.keys = []
        for slot in range(count):
            at, inner = slot // local, slot % local
            fars = self.quarter // local
            side, pair, far = at // (2 * fars), (at // fars) % 2, at % fars
            self.keys.append((me ^ (far * 4 + pair * 2 + side)) * local + inner)

    def heads(self, col_ref, count):
        cols = [col_ref[key] for key in self.keys[:count]]
        found = []
        for slot in range(count):
            best = jnp.int32(slot)
            for earlier in reversed(range(slot)):
                best = jnp.where(cols[earlier] == cols[slot], earlier, best)
            found.append(best)
        return found


def forward(w_ref, at, tok, cot, gu_ref, dh_ref, to):
    two = gu_ref.shape[1]
    gu_ref[to] = dot(w_ref[at, :two], tok, 1, 1)
    dh_ref[to] = dot(w_ref[at, two:], cot, 1, 1)


def backward(grad_ref, at, gu_grad, hidden, tok, cot):
    two = gu_grad.shape[0]
    grad_ref[at, :two] = dot(gu_grad, tok, 1, 0).astype(BF16)
    grad_ref[at, two:] = dot(hidden, cot, 1, 0).astype(BF16)


def bring_kernel(array, out_ref, sem):
    copy = pltpu.make_async_copy(array, out_ref, sem)
    copy.start()
    copy.wait()


def collect_kernel(in_ref, out_row_ref, tokens, cotangent, tok_ref, cot_ref, sems, *, local):
    count, _, block = cot_ref.shape
    slots = Slots(count, local)
    copies = []
    for slot, key in enumerate(slots.keys):
        at = pl.ds(pl.multiple_of(out_row_ref[key] * block, block), block)
        copies.append(pltpu.make_async_copy(cotangent.at[:, at], cot_ref.at[slot], sems.at[slot]))
    for copy in copies:
        copy.start()
    for slot, key in enumerate(slots.keys):
        tok_ref[slot] = tokens[:, pl.ds(pl.multiple_of(in_ref[key] * block, block), block)]
    for copy in copies:
        copy.wait()


def middle(slot, gu, dh, gu_grad, hidden):
    share = dh.shape[1]
    gate, up, grad = gu[slot, :share], gu[slot, share:], dh[slot]
    sig = jax.nn.sigmoid(gate)
    act = gate * sig
    hidden[slot] = (act * up).astype(BF16)
    gu_grad[slot, :share] = (grad * up * sig * (1.0 + gate * (1.0 - sig))).astype(BF16)
    gu_grad[slot, share:] = (grad * act).astype(BF16)


def join(slot, head, gu, dh):
    @pl.when(head != slot)
    def _():
        gu[head] += gu[slot]
        dh[head] += dh[slot]


def first_kernel(w_ref, tok_ref, cot_ref, gu, dh):
    for slot in range(w_ref.shape[0]):
        forward(w_ref, slot, tok_ref[slot], cot_ref[slot], gu, dh, slot)


def second_kernel(cols, w_ref, tok_ref, cot_ref, gu_in, dh_in, gu, dh, gu_grad, hidden, col_ref, sem, *, local):
    del gu_in, dh_in
    copy = pltpu.make_async_copy(cols, col_ref, sem)
    copy.start()
    slots = Slots(gu.shape[0], local)
    for slot in range(slots.quarter, slots.half):
        forward(w_ref, slot - slots.quarter, tok_ref[slot], cot_ref[slot], gu, dh, slot)
    copy.wait()
    heads = slots.heads(col_ref, slots.half)
    for slot in range(1, slots.half):
        join(slot, heads[slot], gu, dh)
    for slot in range(slots.half):
        middle(slot, gu, dh, gu_grad, hidden)


def third_kernel(
    cols,
    w_ref,
    tok_ref,
    cot_ref,
    gu_in,
    dh_in,
    gg_in,
    hid_in,
    grad_ref,
    gu,
    dh,
    gu_grad,
    hidden,
    col_ref,
    sem,
    *,
    local,
):
    del gu_in, dh_in, gg_in, hid_in
    slots = Slots(gu.shape[0], local)
    count, half = slots.count, slots.half
    copy = pltpu.make_async_copy(cols, col_ref, sem)
    copy.start()
    for slot in range(half, count):
        forward(w_ref, slot - half, tok_ref[slot], cot_ref[slot], gu, dh, slot)
    copy.wait()
    heads = slots.heads(col_ref, count)
    shared = jnp.bool_(False)
    for slot in range(half, count):
        shared = shared | (heads[slot] != slot)

    @pl.when(shared)
    def _():
        for slot in range(half, count):
            join(slot, heads[slot], gu, dh)
        for near in range(half):
            changed = heads[half] == near
            for slot in range(half + 1, count):
                changed = changed | (heads[slot] == near)

            @pl.when(changed)
            def _(near=near):
                middle(near, gu, dh, gu_grad, hidden)

    for slot in range(half, count):
        middle(slot, gu, dh, gu_grad, hidden)
    for slot in range(half, count):
        head = heads[slot]
        backward(grad_ref, slot - half, gu_grad[head], hidden[head], tok_ref[slot], cot_ref[slot])


def fourth_kernel(cols, rows_in, near_ref, far_ref, tok_ref, cot_ref, gu_grad, hidden, *rest, ranks, local):
    spread_refs, (grad_ref, total, col_ref, in_ref, sems) = rest[:ranks], rest[ranks:]
    count, two, _ = gu_grad.shape
    block = tok_ref.shape[2]
    copies = [
        pltpu.make_async_copy(cols, col_ref, sems.at[0]),
        pltpu.make_async_copy(rows_in, in_ref, sems.at[1]),
    ]
    for copy in copies:
        copy.start()
    slots = Slots(count, local)
    half = slots.half
    rank = lax.axis_index("mp")
    total[...] = jnp.zeros_like(total)
    for copy in copies:
        copy.wait()
    heads = slots.heads(col_ref, count)
    for slot in range(count):
        weight = near_ref[slot, :two] if slot < half else far_ref[slot - half, :two]
        total[in_ref[slots.keys[slot]]] += dot(gu_grad[heads[slot]], weight, 0, 0)
    per = total.shape[0] // ranks
    for d in range(ranks):
        for r in range(per):
            spread_refs[d][:, r * block : (r + 1) * block] = total[(rank ^ d) * per + r].astype(BF16)
    for slot in range(half):
        head = heads[slot]
        backward(grad_ref, slot, gu_grad[head], hidden[head], tok_ref[slot], cot_ref[slot])


def place_kernel(*refs, ranks):
    pieces, (gate_ref, up_ref, down_ref, whole) = refs[:ranks], refs[ranks:]
    share = pieces[0].shape[1] // 3
    for i in range(gate_ref.shape[0]):
        for part, ref in enumerate((gate_ref, up_ref, down_ref)):
            for d in range(ranks):
                at = pl.multiple_of((lax.axis_index("mp") ^ d) * share, share)
                whole[pl.ds(at, share), :] = pieces[d][i, part * share : (part + 1) * share].astype(F32)
            ref[i] = whole[...] if part == 2 else whole[...].T


def call(kernel, out_shape, spaces, scratch=(), mib=4, flops=0, aliases=None):
    where = {"s": SMEM, "h": HBM, "v": VMEM}
    return pl.pallas_call(
        kernel,
        out_shape=out_shape,
        in_specs=[pl.BlockSpec(memory_space=where[c]) for c in spaces],
        out_specs=jax.tree.map(lambda _: pl.BlockSpec(memory_space=VMEM), out_shape),
        scratch_shapes=list(scratch),
        input_output_aliases=aliases or {},
        compiler_params=pltpu.CompilerParams(vmem_limit_bytes=mib << 20),
        cost_estimate=pl.CostEstimate(flops=flops, bytes_accessed=flops // 256, transcendentals=0) if flops else None,
    )


def outside(x):
    return pltpu.with_memory_space_constraint(x, HBM)


def on_device(tokens, cotangent, gate_blocks, up_blocks, down_blocks, col_block, in_row, out_row):
    token_count, width = tokens.shape
    local, block, _ = gate_blocks.shape
    count = col_block.shape[0]
    groups, ranks = lax.axis_size("dp"), lax.axis_size("mp")
    share = block // ranks
    two, rows = 2 * share, 3 * share
    fars = groups // 4
    quarter = fars * local
    scale = (token_count * groups) ** -0.5
    macs = 2 * token_count * block * rows

    def f32(*dims):
        return jax.ShapeDtypeStruct(dims, F32)

    def bf16(*dims):
        return jax.ShapeDtypeStruct(dims, BF16)

    def along(x, axis, size, d):
        return lax.ppermute(x, axis, [(i, i ^ d) for i in range(size)])

    def over(x, d):
        return along(x, "dp", groups, d)

    def across(x, d):
        return along(x, "mp", ranks, d)

    own = call(
        pack_kernel,
        bf16(local, rows, block),
        "hhh",
        [
            pltpu.VMEM((3, local, block, block), BF16),
            pltpu.VMEM((block, block), F32),
            pltpu.SemaphoreType.DMA((3,)),
        ],
    )(*map(outside, (gate_blocks, up_blocks, down_blocks)))
    across_z = [over(own, 4 * i) for i in range(1, fars)]
    beside_own, beside_next = over(own, 2), over(own, 6)
    column = jnp.concatenate([own] + across_z, axis=0)
    onward = over(jnp.concatenate(across_z[1:], axis=0), 2)
    beside = jnp.concatenate([beside_own, beside_next, onward], axis=0)
    held = call(
        bring_kernel, bf16(token_count, width), "h", [pltpu.SemaphoreType.DMA], 4, macs * quarter
    )(outside(tokens))
    tok, cot = call(
        functools.partial(collect_kernel, local=local),
        [bf16(count, token_count, block)] * 2,
        "ssvh",
        [pltpu.SemaphoreType.DMA((count,))],
        6,
        macs * quarter,
    )(outside(in_row), outside(out_row), held, outside(cotangent))
    cols = outside(col_block)
    sums = [f32(count, two, token_count), f32(count, share, token_count)]
    grads = [bf16(count, two, token_count), bf16(count, share, token_count)]
    gu, dh = call(first_kernel, sums, "vvv", (), 12, macs * quarter)(column, tok, cot)
    beside, gu = lax.optimization_barrier((beside, gu))
    near = jnp.concatenate([column, beside], axis=0)
    far = over(near, 1)
    gu, dh, gu_grad, hidden = call(
        functools.partial(second_kernel, local=local),
        sums + grads,
        "hvvvvv",
        [pltpu.SMEM((count,), jnp.int32), pltpu.SemaphoreType.DMA],
        12,
        macs * quarter,
        {4: 0, 5: 1},
    )(cols, beside, tok, cot, gu, dh)
    grad_parts = bf16(2 * quarter, rows, block)
    far_grad, _, _, gu_grad, hidden = call(
        functools.partial(third_kernel, local=local),
        [grad_parts] + sums + grads,
        "hvvvvvvv",
        [pltpu.SMEM((count,), jnp.int32), pltpu.SemaphoreType.DMA],
        12,
        macs * count,
        {4: 1, 5: 2, 6: 3, 7: 4},
    )(cols, far, tok, cot, gu, dh, gu_grad, hidden)
    *spread, near_grad = call(
        functools.partial(fourth_kernel, ranks=ranks, local=local),
        [bf16(token_count, width // ranks)] * ranks + [grad_parts],
        "hhvvvvvv",
        [
            pltpu.VMEM((width // block, token_count, block), F32),
            pltpu.SMEM((count,), jnp.int32),
            pltpu.SMEM((count,), jnp.int32),
            pltpu.SemaphoreType.DMA((2,)),
        ],
        12,
        macs * count,
    )(cols, outside(in_row), near, far, tok, cot, gu_grad, hidden)

    arrived = [across(spread[d], d) for d in range(1, ranks)]
    chip = near_grad.astype(F32) + over(far_grad, 1).astype(F32)
    onward = over(chip[quarter + 2 * local :].astype(BF16), 2).astype(F32)
    summed = chip[:local]
    for i in range(2, fars):
        piece = chip[i * local : (i + 1) * local] + onward[(i - 2) * local : (i - 1) * local]
        summed = summed + over(piece.astype(BF16), 4 * i).astype(F32)
    for first, d in ((local, 4), (quarter, 2), (quarter + local, 6)):
        summed = summed + over(chip[first : first + local].astype(BF16), d).astype(F32)
    summed = summed * scale
    pieces = [summed] + [across(summed.astype(BF16), d) for d in range(1, ranks)]
    input_grad = spread[0].astype(F32)
    for piece in arrived:
        input_grad = input_grad + piece.astype(F32)
    input_grad, *pieces = lax.optimization_barrier((input_grad.astype(BF16), *pieces))
    gate_grads, up_grads, down_grads = call(
        functools.partial(place_kernel, ranks=ranks),
        [f32(local, block, block)] * 3,
        "v" * ranks,
        [pltpu.VMEM((block, block), F32)],
    )(*pieces)
    return input_grad, gate_grads, up_grads, down_grads


def solution(mesh):
    flat = P("dp", None, None)
    return jax.shard_map(
        on_device,
        mesh=mesh,
        in_specs=(P("dp", None), P("dp", None), flat, flat, flat, P(), P(), P()),
        out_specs=(P("dp", "mp"), flat, flat, flat),
        check_vma=False,
    )
```

time: 45 us -> 43.8 us (0.973)
  Pallas kernels: 10.1 us -> 9.59 us
    pallas_call x6, Pallas kernels: 7.63 us -> 7.11 us  [the longest x1 1.91 us: on_device(): call(functools.partial(collect_kernel, local=local), [bf16(count, token_c...]
  transfers between devices with their start and end apart: 16 -> 16, of which waited for: 6 -> 7; matrix products, arithmetic and copies ran while one was open for 3% -> 3% of each run, Pallas kernels for 14% -> 14%
where the time goes in v5:
time: 43.8 us; the launch traced here: 43.5 us
  starting transfers between devices  20.8 us (47%)
  waiting for transfers between devices  11 us (25%)
  Pallas kernels  9.59 us (22%)
  other arithmetic  1.23 us (3%)
  between operations  0.8 us (2%)
    ppermute x16, starting transfers between devices, along(): return lax.ppermute(x, axis, [(i, i ^ d) for i in range(size)])  20.8 us
    ppermute x16, waiting for transfers between devices, along(): return lax.ppermute(x, axis, [(i, i ^ d) for i in range(size)])  11 us
    pallas_call x1, Pallas kernels, on_device(): call(functools.partial(collect_kernel, local=local), [bf16(count, token_c...  1.91 us
    pallas_call x1, Pallas kernels, on_device(): call(functools.partial(fourth_kernel, ranks=ranks, local=local), [bf16(to...  1.69 us
    pallas_call x1, Pallas kernels, on_device(): call(functools.partial(third_kernel, local=local), [grad_parts] + sums +...  1.6 us
    pallas_call x1, Pallas kernels, on_device(): call(bring_kernel, bf16(token_count, width), 'h', [pltpu.SemaphoreType.DM...  1.28 us
    pallas_call x1, Pallas kernels, on_device(): call(pack_kernel, bf16(local, rows, block), 'hhh', [pltpu.VMEM((3, local,...  1.01 us
    pallas_call x1, Pallas kernels, on_device(): call(functools.partial(second_kernel, local=local), sums + grads, 'hvvvvv...  0.99 us
  transfers between devices with their start and end apart: 16, of which 7 were waited for; matrix products, arithmetic and copies ran while one was open for 3% of the time, Pallas kernels for 14%

profile of v5, /device:TPU:0, one launch (start us, length us, event | category | flops | bytes accessed | tf_op | source)
XLA Modules:
  0.0 43.5 jit_solution(12727037523149367990)
XLA Ops:
  0.6 1.0 %shard_map.111 = bf16[1,192,128]{2,1,0:T(8,128)(2,1)S(1)} custom-call(bf16[1,128,128]{2,1,0:T(8,128)(2,1)} %gate_ref.1, bf16[1,128,128]{2,1,0:T(8,128)(2,1)} %up_ref.1, bf16[1,128,128]{2,1,0:T(8,128)(2,1)} %down_ref.1), custom_call_target="tpu_custom_call" | custom-call | tf_op jit(solution)/shard_map/pallas_call | solution.py:268
  1.6 4.1 %collective-permute-start.4 = (bf16[1,192,128]{2,1,0:T(8,128)(2,1)S(1)}, bf16[1,192,128]{2,1,0:T(8,128)(2,1)S(1)}, u32[]{:S(2)}, u32[]{:S(2)}) collective-permute-start(bf16[1,192,128]{2,1,0:T(8,128)(2,1)S(1)} %shard_map.111), channel_id=1, source_target_pairs={{0,12},{2,14},{4,8},{6,10},{8,4},{10,6},{12,0},{14,2},{16,28},{18,... | collective-permute-start | bytes 147464 | tf_op jit(solution)/shard_map/ppermute | solution.py:260
  6.2 2.5 %collective-permute-start.2 = (bf16[1,192,128]{2,1,0:T(8,128)(2,1)S(1)}, bf16[1,192,128]{2,1,0:T(8,128)(2,1)S(1)}, u32[]{:S(2)}, u32[]{:S(2)}) collective-permute-start(bf16[1,192,128]{2,1,0:T(8,128)(2,1)S(1)} %shard_map.111), channel_id=1, source_target_pairs={{0,24},{2,26},{4,28},{6,30},{8,16},{10,18},{12,20},{14,22},{16,8},... | collective-permute-start | bytes 147464 | tf_op jit(solution)/shard_map/ppermute | solution.py:260
  8.8 1.8 %collective-permute-start = (bf16[1,192,128]{2,1,0:T(8,128)(2,1)S(1)}, bf16[1,192,128]{2,1,0:T(8,128)(2,1)S(1)}, u32[]{:S(2)}, u32[]{:S(2)}) collective-permute-start(bf16[1,192,128]{2,1,0:T(8,128)(2,1)S(1)} %shard_map.111), channel_id=1, source_target_pairs={{0,8},{2,10},{4,12},{6,14},{8,0},{10,2},{12,4},{14,6},{16,24},{18,... | collective-permute-start | bytes 147464 | tf_op jit(solution)/shard_map/ppermute | solution.py:260
  10.6 1.3 %shard_map.112.tokens = bf16[144,4096]{1,0:T(8,128)(2,1)S(1)} custom-call(bf16[144,4096]{1,0:T(8,128)(2,1)} %array.1), custom_call_target="tpu_custom_call" | custom-call | flops 28311552 | bytes 110592 | tf_op jit(solution)/shard_map/pallas_call | solution.py:283
  11.9 1.9 %shard_map.113 = (bf16[16,144,128]{2,1,0:T(8,128)(2,1)S(1)}, bf16[16,144,128]{2,1,0:T(8,128)(2,1)S(1)}) custom-call(s32[16]{0:T(128)} %rows_in.1, s32[16]{0:T(128)} %out_row_ref.1, bf16[144,4096]{1,0:T(8,128)(2,1)S(1)} %shard_map.112.tokens, bf16[144,4096]{1,0:T(8,128)(2,1)} %cotangent.1), custom_call_target="tpu_custom_call" | custom-call | flops 28311552 | bytes 110592 | tf_op jit(solution)/shard_map/pallas_call | solution.py:286
  14.2 1.6 %collective-permute-start.5 = (bf16[2,192,128]{2,1,0:T(8,128)(2,1)S(1)}, bf16[2,192,128]{2,1,0:T(8,128)(2,1)S(1)}, u32[]{:S(2)}, u32[]{:S(2)}) collective-permute-start(bf16[2,192,128]{2,1,0:T(8,128)(2,1)S(1)} %pad_maximum_fusion.2), channel_id=1, source_target_pairs={{0,4},{2,6},{4,0},{6,2},{8,12},{10,14},{12,8},{14,10},{16,20},{18,... | collective-permute-start | bytes 294920 | tf_op jit(solution)/shard_map/ppermute | solution.py:260
  16.2 2.7 %collective-permute-done.5 = bf16[2,192,128]{2,1,0:T(8,128)(2,1)S(1)} collective-permute-done((bf16[2,192,128]{2,1,0:T(8,128)(2,1)S(1)}, bf16[2,192,128]{2,1,0:T(8,128)(2,1)S(1)}, u32[]{:S(2)}, u32[]{:S(2)}) %collective-permute-start.5) | collective-permute-done | bytes 98336 | tf_op jit(solution)/shard_map/ppermute | solution.py:260
  19.1 1.0 %shard_map.115 = (f32[16,128,144]{2,1,0:T(8,128)S(1)}, f32[16,64,144]{2,1,0:T(8,128)S(1)}, bf16[16,128,144]{2,1,0:T(8,128)(2,1)S(1)}, bf16[16,64,144]{2,1,0:T(8,128)(2,1)S(1)}) custom-call(s32[16]{0:T(128)} %cols.5, bf16[4,192,128]{2,1,0:T(8,128)(2,1)S(1)} %pad_maximum_fusion.w_ref, ...), custom_call_target="tpu_custom_call", output_to_operand_aliasing={{0}: (4, {}), {1}: (5, {})} | custom-call | flops 28311552 | bytes 110592 | tf_op jit(solution)/shard_map/pallas_call | solution.py:301
  20.1 0.7 %collective-permute-done.6.w_ref.far_ref = bf16[8,192,128]{2,1,0:T(8,128)(2,1)S(1)} collective-permute-done((bf16[8,192,128]{2,1,0:T(8,128)(2,1)S(1)}, bf16[8,192,128]{2,1,0:T(8,128)(2,1)S(1)}, u32[]{:S(2)}, u32[]{:S(2)}) %collective-permute-start.6) | collective-permute-done | bytes 393248 | tf_op jit(solution)/shard_map/ppermute | solution.py:260
  20.8 1.6 %shard_map.116 = (bf16[8,192,128]{2,1,0:T(8,128)(2,1)S(1)}, f32[16,128,144]{2,1,0:T(8,128)S(1)}, f32[16,64,144]{2,1,0:T(8,128)S(1)}, bf16[16,128,144]{2,1,0:T(8,128)(2,1)S(1)}, bf16[16,64,144]{2,1,0:T(8,128)(2,1)S(1)}) custom-call(s32[16]{0:T(128)} %cols.5, ...), custom_call_target="tpu_custom_call", output_to_operand_aliasing={{1}: (4, {}), {2}: (5, {}), {3}: (6, {}), {4}: (7, {})} | custom-call | flops 113246208 | bytes 442368 | tf_op jit(solution)/shard_map/pallas_call | solution.py:311
  22.6 1.7 %shard_map.117 = (bf16[144,2048]{1,0:T(8,128)(2,1)S(1)}, bf16[144,2048]{1,0:T(8,128)(2,1)S(1)}, bf16[8,192,128]{2,1,0:T(8,128)(2,1)S(1)}) custom-call(s32[16]{0:T(128)} %cols.5, s32[16]{0:T(128)} %rows_in.1, bf16[8,192,128]{2,1,0:T(8,128)(2,1)S(1)} %constant_dynamic-update-slice_fusion.near_ref, ...), custom_call_target="tpu_custom_call" | custom-call | flops 113246208 | bytes 442368 | tf_op jit(solution)/shard_map/pallas_call | solution.py:320
  24.3 1.6 %collective-permute-start.7 = (bf16[144,2048]{1,0:T(8,128)(2,1)S(1)}, bf16[144,2048]{1,0:T(8,128)(2,1)S(1)}, u32[]{:S(2)}, u32[]{:S(2)}) collective-permute-start(bf16[144,2048]{1,0:T(8,128)(2,1)S(1)} %get-tuple-element.39), channel_id=1, source_target_pairs={{0,1},{1,0},{2,3},{3,2},{4,5},{5,4},{6,7},{7,6},{8,9},{9,8},{10,11... | collective-permute-start | bytes 1769480 | tf_op jit(solution)/shard_map/ppermute | solution.py:260
  26.0 1.6 %collective-permute-start.9 = (bf16[2,192,128]{2,1,0:T(8,128)(2,1)S(1)}, bf16[2,192,128]{2,1,0:T(8,128)(2,1)S(1)}, u32[]{:S(2)}, u32[]{:S(2)}) collective-permute-start(bf16[2,192,128]{2,1,0:T(8,128)(2,1)S(1)} %slice.42), channel_id=1, source_target_pairs={{0,4},{2,6},{4,0},{6,2},{8,12},{10,14},{12,8},{14,10},{16,20},{18,... | collective-permute-start | bytes 294920 | tf_op jit(solution)/shard_map/ppermute | solution.py:260
  27.9 1.7 %collective-permute-start.14 = (bf16[1,192,128]{2,1,0:T(8,128)(2,1)S(1)}, bf16[1,192,128]{2,1,0:T(8,128)(2,1)S(1)}, u32[]{:S(2)}, u32[]{:S(2)}) collective-permute-start(bf16[1,192,128]{2,1,0:T(8,128)(2,1)S(1)} %get-tuple-element.55), channel_id=1, source_target_pairs={{0,12},{2,14},{4,8},{6,10},{8,4},{10,6},{12,0},{14,2},{16,28},{18,... | collective-permute-start | bytes 147464 | tf_op jit(solution)/shard_map/ppermute | solution.py:260
  29.6 1.5 %collective-permute-start.13 = (bf16[1,192,128]{2,1,0:T(8,128)(2,1)S(1)}, bf16[1,192,128]{2,1,0:T(8,128)(2,1)S(1)}, u32[]{:S(2)}, u32[]{:S(2)}) collective-permute-start(bf16[1,192,128]{2,1,0:T(8,128)(2,1)S(1)} %get-tuple-element.56), channel_id=1, source_target_pairs={{0,4},{2,6},{4,0},{6,2},{8,12},{10,14},{12,8},{14,10},{16,20},{18,... | collective-permute-start | bytes 147464 | tf_op jit(solution)/shard_map/ppermute | solution.py:260
  31.2 1.4 %collective-permute-start.10 = (bf16[1,192,128]{2,1,0:T(8,128)(2,1)S(1)}, bf16[1,192,128]{2,1,0:T(8,128)(2,1)S(1)}, u32[]{:S(2)}, u32[]{:S(2)}) collective-permute-start(bf16[1,192,128]{2,1,0:T(8,128)(2,1)S(1)} %get-tuple-element.50), channel_id=1, source_target_pairs={{0,16},{2,18},{4,20},{6,22},{8,24},{10,26},{12,28},{14,30},{16,0},... | collective-permute-start | bytes 147464 | tf_op jit(solution)/shard_map/ppermute | solution.py:260
  32.6 1.3 %collective-permute-start.11 = (bf16[1,192,128]{2,1,0:T(8,128)(2,1)S(1)}, bf16[1,192,128]{2,1,0:T(8,128)(2,1)S(1)}, u32[]{:S(2)}, u32[]{:S(2)}) collective-permute-start(bf16[1,192,128]{2,1,0:T(8,128)(2,1)S(1)} %get-tuple-element.51), channel_id=1, source_target_pairs={{0,24},{2,26},{4,28},{6,30},{8,16},{10,18},{12,20},{14,22},{16,8},... | collective-permute-start | bytes 147464 | tf_op jit(solution)/shard_map/ppermute | solution.py:260
  33.9 3.1 %collective-permute-done.10 = bf16[1,192,128]{2,1,0:T(8,128)(2,1)S(1)} collective-permute-done((bf16[1,192,128]{2,1,0:T(8,128)(2,1)S(1)}, bf16[1,192,128]{2,1,0:T(8,128)(2,1)S(1)}, u32[]{:S(2)}, u32[]{:S(2)}) %collective-permute-start.10) | collective-permute-done | bytes 49184 | tf_op jit(solution)/shard_map/ppermute | solution.py:260
  37.0 1.5 %collective-permute-done.11 = bf16[1,192,128]{2,1,0:T(8,128)(2,1)S(1)} collective-permute-done((bf16[1,192,128]{2,1,0:T(8,128)(2,1)S(1)}, bf16[1,192,128]{2,1,0:T(8,128)(2,1)S(1)}, u32[]{:S(2)}, u32[]{:S(2)}) %collective-permute-start.11) | collective-permute-done | bytes 49184 | tf_op jit(solution)/shard_map/ppermute | solution.py:260
  39.1 1.4 %collective-permute-done.7 = bf16[144,2048]{1,0:T(8,128)(2,1)S(1)} collective-permute-done((bf16[144,2048]{1,0:T(8,128)(2,1)S(1)}, bf16[144,2048]{1,0:T(8,128)(2,1)S(1)}, u32[]{:S(2)}, u32[]{:S(2)}) %collective-permute-start.7) | collective-permute-done | bytes 589856 | tf_op jit(solution)/shard_map/ppermute | solution.py:260
  40.5 1.0 %add_convert_fusion = bf16[144,2048]{1,0:T(8,128)(2,1)} fusion(bf16[144,2048]{1,0:T(8,128)(2,1)S(1)} %collective-permute-done.7, bf16[144,2048]{1,0:T(8,128)(2,1)S(1)} %get-tuple-element.38), kind=kLoop, calls=%fused_computation | loop fusion | flops 1179648 | bytes 1769472 | tf_op jit(solution)/shard_map/convert_element_type | solution.py:348
  41.5 1.2 %collective-permute-done.15.refs_1_ = bf16[1,192,128]{2,1,0:T(8,128)(2,1)S(1)} collective-permute-done((bf16[1,192,128]{2,1,0:T(8,128)(2,1)S(1)}, bf16[1,192,128]{2,1,0:T(8,128)(2,1)S(1)}, u32[]{:S(2)}, u32[]{:S(2)}) %collective-permute-start.15) | collective-permute-done | bytes 49184 | tf_op jit(solution)/shard_map/ppermute | solution.py:260
  42.7 0.8 %shard_map.118 = (f32[1,128,128]{2,1,0:T(8,128)}, f32[1,128,128]{2,1,0:T(8,128)}, f32[1,128,128]{2,1,0:T(8,128)}) custom-call(f32[1,192,128]{2,1,0:T(8,128)S(1)} %get-tuple-element.43.refs_0_, bf16[1,192,128]{2,1,0:T(8,128)(2,1)S(1)} %collective-permute-done.15.refs_1_), custom_call_target="tpu_custom_call" | custom-call | tf_op jit(solution)/shard_map/pallas_call | solution.py:349
  (31 shorter events, 2.9 us)
Async XLA Ops:
  1.6 14.6 %collective-permute-start.4 = (bf16[1,192,128]{2,1,0:T(8,128)(2,1)S(1)}, bf16[1,192,128]{2,1,0:T(8,128)(2,1)S(1)}, u32[]{:S(2)}, u32[]{:S(2)}) collective-permute-start(bf16[1,192,128]{2,1,0:T(8,128)(2,1)S(1)} %shard_map.111), channel_id=1, source_target_pairs={{0,12},{2,14},{4,8},{6,10},{8,4},{10,6},{12,0},{14,2},{16,28},{18,... | collective-permute-start | bytes 147464 | tf_op jit(solution)/shard_map/ppermute | solution.py:260
  5.7 10.5 %collective-permute-start.3 = (bf16[1,192,128]{2,1,0:T(8,128)(2,1)S(1)}, bf16[1,192,128]{2,1,0:T(8,128)(2,1)S(1)}, u32[]{:S(2)}, u32[]{:S(2)}) collective-permute-start(bf16[1,192,128]{2,1,0:T(8,128)(2,1)S(1)} %shard_map.111), channel_id=1, source_target_pairs={{0,4},{2,6},{4,0},{6,2},{8,12},{10,14},{12,8},{14,10},{16,20},{18,... | collective-permute-start | bytes 147464 | tf_op jit(solution)/shard_map/ppermute | solution.py:260
  6.2 7.6 %collective-permute-start.2 = (bf16[1,192,128]{2,1,0:T(8,128)(2,1)S(1)}, bf16[1,192,128]{2,1,0:T(8,128)(2,1)S(1)}, u32[]{:S(2)}, u32[]{:S(2)}) collective-permute-start(bf16[1,192,128]{2,1,0:T(8,128)(2,1)S(1)} %shard_map.111), channel_id=1, source_target_pairs={{0,24},{2,26},{4,28},{6,30},{8,16},{10,18},{12,20},{14,22},{16,8},... | collective-permute-start | bytes 147464 | tf_op jit(solution)/shard_map/ppermute | solution.py:260
  8.7 5.5 %collective-permute-start.1 = (bf16[1,192,128]{2,1,0:T(8,128)(2,1)S(1)}, bf16[1,192,128]{2,1,0:T(8,128)(2,1)S(1)}, u32[]{:S(2)}, u32[]{:S(2)}) collective-permute-start(bf16[1,192,128]{2,1,0:T(8,128)(2,1)S(1)} %shard_map.111), channel_id=1, source_target_pairs={{0,16},{2,18},{4,20},{6,22},{8,24},{10,26},{12,28},{14,30},{16,0},... | collective-permute-start | bytes 147464 | tf_op jit(solution)/shard_map/ppermute | solution.py:260
  8.8 7.0 %collective-permute-start = (bf16[1,192,128]{2,1,0:T(8,128)(2,1)S(1)}, bf16[1,192,128]{2,1,0:T(8,128)(2,1)S(1)}, u32[]{:S(2)}, u32[]{:S(2)}) collective-permute-start(bf16[1,192,128]{2,1,0:T(8,128)(2,1)S(1)} %shard_map.111), channel_id=1, source_target_pairs={{0,8},{2,10},{4,12},{6,14},{8,0},{10,2},{12,4},{14,6},{16,24},{18,... | collective-permute-start | bytes 147464 | tf_op jit(solution)/shard_map/ppermute | solution.py:260
  14.2 4.7 %collective-permute-start.5 = (bf16[2,192,128]{2,1,0:T(8,128)(2,1)S(1)}, bf16[2,192,128]{2,1,0:T(8,128)(2,1)S(1)}, u32[]{:S(2)}, u32[]{:S(2)}) collective-permute-start(bf16[2,192,128]{2,1,0:T(8,128)(2,1)S(1)} %pad_maximum_fusion.2), channel_id=1, source_target_pairs={{0,4},{2,6},{4,0},{6,2},{8,12},{10,14},{12,8},{14,10},{16,20},{18,... | collective-permute-start | bytes 294920 | tf_op jit(solution)/shard_map/ppermute | solution.py:260
  19.0 1.8 %collective-permute-start.6 = (bf16[8,192,128]{2,1,0:T(8,128)(2,1)S(1)}, bf16[8,192,128]{2,1,0:T(8,128)(2,1)S(1)}, u32[]{:S(2)}, u32[]{:S(2)}) collective-permute-start(bf16[8,192,128]{2,1,0:T(8,128)(2,1)S(1)} %constant_dynamic-update-slice_fusion.near_ref), channel_id=1, source_target_pairs={{0,2},{2,0},{4,6},{6,4},{8,10},{10,8},{12,14},{14,12},{16,18},{18,... | collective-permute-start | bytes 1179656 | tf_op jit(solution)/shard_map/ppermute | solution.py:260
  22.4 3.5 %collective-permute-start.8 = (bf16[8,192,128]{2,1,0:T(8,128)(2,1)S(1)}, bf16[8,192,128]{2,1,0:T(8,128)(2,1)S(1)}, u32[]{:S(2)}, u32[]{:S(2)}) collective-permute-start(bf16[8,192,128]{2,1,0:T(8,128)(2,1)S(1)} %get-tuple-element.41), channel_id=1, source_target_pairs={{0,2},{2,0},{4,6},{6,4},{8,10},{10,8},{12,14},{14,12},{16,18},{18,... | collective-permute-start | bytes 1179656 | tf_op jit(solution)/shard_map/ppermute | solution.py:260
  24.3 16.2 %collective-permute-start.7 = (bf16[144,2048]{1,0:T(8,128)(2,1)S(1)}, bf16[144,2048]{1,0:T(8,128)(2,1)S(1)}, u32[]{:S(2)}, u32[]{:S(2)}) collective-permute-start(bf16[144,2048]{1,0:T(8,128)(2,1)S(1)} %get-tuple-element.39), channel_id=1, source_target_pairs={{0,1},{1,0},{2,3},{3,2},{4,5},{5,4},{6,7},{7,6},{8,9},{9,8},{10,11... | collective-permute-start | bytes 1769480 | tf_op jit(solution)/shard_map/ppermute | solution.py:260
  26.0 5.2 %collective-permute-start.9 = (bf16[2,192,128]{2,1,0:T(8,128)(2,1)S(1)}, bf16[2,192,128]{2,1,0:T(8,128)(2,1)S(1)}, u32[]{:S(2)}, u32[]{:S(2)}) collective-permute-start(bf16[2,192,128]{2,1,0:T(8,128)(2,1)S(1)} %slice.42), channel_id=1, source_target_pairs={{0,4},{2,6},{4,0},{6,2},{8,12},{10,14},{12,8},{14,10},{16,20},{18,... | collective-permute-start | bytes 294920 | tf_op jit(solution)/shard_map/ppermute | solution.py:260
  27.6 5.0 %collective-permute-start.12 = (bf16[1,192,128]{2,1,0:T(8,128)(2,1)S(1)}, bf16[1,192,128]{2,1,0:T(8,128)(2,1)S(1)}, u32[]{:S(2)}, u32[]{:S(2)}) collective-permute-start(bf16[1,192,128]{2,1,0:T(8,128)(2,1)S(1)} %get-tuple-element.54), channel_id=1, source_target_pairs={{0,8},{2,10},{4,12},{6,14},{8,0},{10,2},{12,4},{14,6},{16,24},{18,... | collective-permute-start | bytes 147464 | tf_op jit(solution)/shard_map/ppermute | solution.py:260
  27.9 6.0 %collective-permute-start.14 = (bf16[1,192,128]{2,1,0:T(8,128)(2,1)S(1)}, bf16[1,192,128]{2,1,0:T(8,128)(2,1)S(1)}, u32[]{:S(2)}, u32[]{:S(2)}) collective-permute-start(bf16[1,192,128]{2,1,0:T(8,128)(2,1)S(1)} %get-tuple-element.55), channel_id=1, source_target_pairs={{0,12},{2,14},{4,8},{6,10},{8,4},{10,6},{12,0},{14,2},{16,28},{18,... | collective-permute-start | bytes 147464 | tf_op jit(solution)/shard_map/ppermute | solution.py:260
  29.6 4.3 %collective-permute-start.13 = (bf16[1,192,128]{2,1,0:T(8,128)(2,1)S(1)}, bf16[1,192,128]{2,1,0:T(8,128)(2,1)S(1)}, u32[]{:S(2)}, u32[]{:S(2)}) collective-permute-start(bf16[1,192,128]{2,1,0:T(8,128)(2,1)S(1)} %get-tuple-element.56), channel_id=1, source_target_pairs={{0,4},{2,6},{4,0},{6,2},{8,12},{10,14},{12,8},{14,10},{16,20},{18,... | collective-permute-start | bytes 147464 | tf_op jit(solution)/shard_map/ppermute | solution.py:260
  31.2 5.8 %collective-permute-start.10 = (bf16[1,192,128]{2,1,0:T(8,128)(2,1)S(1)}, bf16[1,192,128]{2,1,0:T(8,128)(2,1)S(1)}, u32[]{:S(2)}, u32[]{:S(2)}) collective-permute-start(bf16[1,192,128]{2,1,0:T(8,128)(2,1)S(1)} %get-tuple-element.50), channel_id=1, source_target_pairs={{0,16},{2,18},{4,20},{6,22},{8,24},{10,26},{12,28},{14,30},{16,0},... | collective-permute-start | bytes 147464 | tf_op jit(solution)/shard_map/ppermute | solution.py:260
  32.6 5.9 %collective-permute-start.11 = (bf16[1,192,128]{2,1,0:T(8,128)(2,1)S(1)}, bf16[1,192,128]{2,1,0:T(8,128)(2,1)S(1)}, u32[]{:S(2)}, u32[]{:S(2)}) collective-permute-start(bf16[1,192,128]{2,1,0:T(8,128)(2,1)S(1)} %get-tuple-element.51), channel_id=1, source_target_pairs={{0,24},{2,26},{4,28},{6,30},{8,16},{10,18},{12,20},{14,22},{16,8},... | collective-permute-start | bytes 147464 | tf_op jit(solution)/shard_map/ppermute | solution.py:260
  38.5 4.2 %collective-permute-start.15 = (bf16[1,192,128]{2,1,0:T(8,128)(2,1)S(1)}, bf16[1,192,128]{2,1,0:T(8,128)(2,1)S(1)}, u32[]{:S(2)}, u32[]{:S(2)}) collective-permute-start(bf16[1,192,128]{2,1,0:T(8,128)(2,1)S(1)} %get-tuple-element.48), channel_id=1, source_target_pairs={{0,1},{1,0},{2,3},{3,2},{4,5},{5,4},{6,7},{7,6},{8,9},{9,8},{10,11... | collective-permute-start | bytes 147464 | tf_op jit(solution)/shard_map/ppermute | solution.py:260
